TPU v7x, 128 devices: a whole 4x4x4 slice. The times are simulated.
128 devices in a mesh: req: 4 (over z), seq: 32 (over x, y, core).
Axes of the slice: x: 4, y: 4, z: 4, core: 2. Of those that a mesh axis runs over, the one named last changes fastest.
Arguments:
- tokens: bfloat16 [4, 2048, 3584], P('req', 'seq'), may hold values from -6 to 6
- w_z: bfloat16 [3584, 7168], P('req', 'seq')
- w_x: bfloat16 [3584, 7168], P('req', 'seq'), may hold values from -0.09375 to 0.09375
- w_bc: bfloat16 [3584, 256], replicated, may hold values from -0.09375 to 0.09375
- w_dt: bfloat16 [3584, 112], replicated, may hold values from -0.09375 to 0.09375
- dt_bias: float32 [112], replicated, may hold values from -2 to 0
- a_rate: float32 [112], replicated, may hold values from 0.00024414062 to 0.2
- conv_weight: float32 [4, 7424], replicated, may hold values from -3 to 3
- conv_bias: float32 [7424], replicated, may hold values from -3 to 3
- d_skip: float32 [112], replicated, may hold values from 0.5 to 1.5
- norm_gain: float32 [7168], replicated, may hold values from 0.5 to 1.5
- lengths: int32 [4], P('req'), may hold values from 512 to 2048, as said below
Outputs:
- mixed: bfloat16 [4, 2048, 7168], P('req', 'seq')
Inputs may be any that keep to these rules, and one draw needn't show every extreme that they name: `lengths`: each prompt has at least 512 valid positions, and the longest fills all 2048.
All inputs are finite; a program needn't handle non-finite values.
Results may differ from a plain program's by a relative error of at most 0.0055.
Values may be sent and summed in bfloat16 or wider, within the bound.
No kernel may reach another device: no remote copies, remote signals or barrier semaphores. Data moves between devices by JAX's collectives and lax.ppermute only.
A program may use at most 320 MiB of HBM per device.

v0:
```python
import jax
import jax.numpy as jnp
from jax import lax
from jax.sharding import PartitionSpec as P

STATE = 64
GROUPS = 2


PRECISE = lax.Precision.HIGHEST


def from_behind(block, axis, distance):
    devices = range(lax.axis_size(axis))
    route = [(i - distance, i) for i in devices if i - distance in devices]
    return lax.ppermute(block, axis, route)


def prefix(shard, axis, combine, identity):
    size, position = (lax.axis_size(axis), lax.axis_index(axis))
    everything = jax.tree.map(lambda part: lax.all_gather(part, axis), shard)
    start = jax.tree.map(
        lambda part, zero: jnp.broadcast_to(jnp.asarray(zero, part.dtype), part.shape),
        shard,
        identity,
    )

    def hop(k, before):
        reached = k < position
        new = combine(before, jax.tree.map(lambda part: part[k], everything))
        return jax.tree.map(lambda a, b: jnp.where(reached, a, b), new, before)

    return lax.fori_loop(0, size, hop, start)


def local_block(x_heads, b_proj, c_proj, step_size, log_decay):
    per_group = x_heads.shape[1] // b_proj.shape[1]
    block_len = x_heads.shape[0]
    running = jnp.cumsum(log_decay, axis=0)
    causal_mask = jnp.arange(block_len)[:, None] >= jnp.arange(block_len)[None, :]
    gaps = running.T[:, :, None] - running.T[:, None, :]
    decay_mask = jnp.where(causal_mask[None], jnp.exp(jnp.minimum(gaps, 0.0)), 0.0)
    affinity = jnp.einsum("ign,jgn->gij", c_proj, b_proj, precision=PRECISE)
    mixing = decay_mask * jnp.repeat(affinity, per_group, axis=0) * step_size.T[:, None, :]
    intra_out = jnp.einsum("hij,jhp->ihp", mixing, x_heads, precision=PRECISE)
    b_heads = jnp.repeat(b_proj, per_group, axis=1)
    tail_weight = jnp.exp(running[-1][None, :] - running) * step_size
    block_state = jnp.einsum(
        "jhp,jhn->hpn", x_heads * tail_weight[:, :, None], b_heads, precision=PRECISE
    )
    return (intra_out, block_state, running)


def finish_block(
    x_heads, c_proj, running, intra_out, state_in, gate_in, d_skip, norm_gain, valid_rows
):
    per_group = x_heads.shape[1] // c_proj.shape[1]
    num_rows = x_heads.shape[0]
    inner_width = norm_gain.shape[0]
    c_heads = jnp.repeat(c_proj, per_group, axis=1)
    carried = jnp.exp(running)[:, :, None] * jnp.einsum(
        "ihn,hpn->ihp", c_heads, state_in, precision=PRECISE
    )
    result = intra_out + carried + d_skip[None, :, None] * x_heads
    gated = result.reshape(num_rows, inner_width) * jax.nn.silu(gate_in.astype(jnp.float32))
    grouped = gated.reshape(num_rows, GROUPS, inner_width // GROUPS)
    inv_scale = lax.rsqrt(jnp.mean(grouped * grouped, axis=2, keepdims=True) + 1e-05)
    normed = (grouped * inv_scale).reshape(num_rows, inner_width) * norm_gain[None, :]
    return jnp.where(valid_rows[:, None], normed, 0.0).astype(jnp.bfloat16)


def combine_states(earlier_part, later_part):
    return (
        earlier_part[0] + later_part[0],
        jnp.exp(later_part[0])[:, None, None] * earlier_part[1] + later_part[1],
    )


def position_mix(
    stacked, bc_proj, dt_raw, dt_bias, a_rate, conv_weight, conv_bias, d_skip, norm_gain, lengths
):
    regrouped = lax.all_to_all(stacked, "seq", split_axis=0, concat_axis=2, tiled=True)
    gate_in = regrouped[:, 0]
    x_in = regrouped[:, 1]
    num_rows = gate_in.shape[0]
    inner_width = norm_gain.shape[0]
    num_heads = a_rate.shape[0]
    head_size = inner_width // num_heads
    conv_taps = conv_weight.shape[0]
    proj_width = bc_proj.shape[1] // 2
    xbc = jnp.concatenate([x_in, bc_proj], axis=1)
    rim_rows = from_behind(xbc[num_rows - (conv_taps - 1) :], "seq", 1)
    padded = jnp.concatenate([rim_rows, xbc], axis=0).astype(jnp.float32)
    conv_sum = conv_bias[None, :] + jnp.zeros(xbc.shape, jnp.float32)
    for offset in range(conv_taps):
        conv_sum = conv_sum + conv_weight[offset][None, :] * padded[offset : offset + num_rows]
    conved = lax.optimization_barrier(jax.nn.silu(conv_sum).astype(jnp.bfloat16)).astype(
        jnp.float32
    )
    x_heads = conved[:, :inner_width].reshape(num_rows, num_heads, head_size)
    b_proj = conved[:, inner_width : inner_width + proj_width].reshape(num_rows, GROUPS, STATE)
    c_proj = conved[:, inner_width + proj_width :].reshape(num_rows, GROUPS, STATE)
    step_size = jax.nn.softplus(dt_raw.astype(jnp.float32) + dt_bias[None, :])
    log_decay = -step_size * a_rate[None, :]
    first_row = lax.axis_index("seq") * num_rows
    valid_rows = first_row + jnp.arange(num_rows, dtype=jnp.int32) < lengths[0]
    intra_out, block_state, running = local_block(x_heads, b_proj, c_proj, step_size, log_decay)
    total_log = running[-1]
    identity = (jnp.zeros_like(total_log), jnp.zeros_like(block_state))
    carried_log, state_in = prefix((total_log, block_state), "seq", combine_states, identity)
    return finish_block(
        x_heads, c_proj, running, intra_out, state_in, gate_in, d_skip, norm_gain, valid_rows
    )


def local(
    tokens,
    w_z,
    w_x,
    w_bc,
    w_dt,
    dt_bias,
    a_rate,
    conv_weight,
    conv_bias,
    d_skip,
    norm_gain,
    lengths,
):
    own_rows = tokens[0]
    z_columns, x_columns = (
        lax.all_gather(w_z, "req", axis=0, tiled=True),
        lax.all_gather(w_x, "req", axis=0, tiled=True),
    )
    shard_piece = lax.all_gather(own_rows, "seq", axis=0, tiled=True)
    gate_part = jnp.dot(shard_piece, z_columns, preferred_element_type=jnp.float32).astype(
        jnp.bfloat16
    )
    input_part = jnp.dot(shard_piece, x_columns, preferred_element_type=jnp.float32).astype(
        jnp.bfloat16
    )
    stacked = jnp.stack([gate_part, input_part], axis=1)
    bc_proj = jnp.dot(own_rows, w_bc, preferred_element_type=jnp.float32).astype(jnp.bfloat16)
    dt_raw = jnp.dot(own_rows, w_dt, preferred_element_type=jnp.float32).astype(jnp.bfloat16)
    operands = (
        stacked,
        bc_proj,
        dt_raw,
        dt_bias,
        a_rate,
        conv_weight,
        conv_bias,
        d_skip,
        norm_gain,
        lengths,
    )
    mixed = position_mix(*operands)
    return mixed[None]


def solution(mesh):
    placed = (
        P("req", "seq", None),
        P("req", "seq"),
        P("req", "seq"),
        P(),
        P(),
        P(),
        P(),
        P(),
        P(),
        P(),
        P(),
        P("req"),
    )
    return jax.shard_map(
        local, mesh=mesh, in_specs=placed, out_specs=P("req", "seq", None), check_vma=False
    )
```

profile of v0, /device:TPU:1, one launch (start us, length us, event | category | flops | bytes accessed | tf_op | source)
XLA Modules:
  0.0 760.8 jit_solution(18271068102787974957)
XLA Ops:
  8.7 30.6 %all-gather.10.cloned.1.call-done = bf16[3584,224]{0,1:T(8,128)(2,1)} async-done(((bf16[896,224]{0,1:T(8,128)(2,1)}), bf16[3584,224]{0,1:T(8,128)(2,1)}) %all-gather.10.cloned.1.call-update) | async-done | bytes 1605648 | tf_op jit(solution)/shard_map/all_gather | solution.py:133
  39.3 70.1 %all-gather.12.cloned.1.call-done = bf16[1,2048,3584]{2,1,0:T(8,128)(2,1)} async-done(((bf16[1,64,3584]{2,1,0:T(8,128)(2,1)}), bf16[1,2048,3584]{2,1,0:T(8,128)(2,1)}) %all-gather.12.cloned.1.call-update) | async-done | bytes 14680080 | tf_op jit(solution)/shard_map/all_gather | solution.py:135
  109.4 10.0 %fusion.16 = bf16[2048,1,224]{0,2,1:T(8,128)(2,1)S(1)} fusion(bf16[3584,224]{0,1:T(8,128)(2,1)} %all-gather.10.cloned.1.call-done, bf16[1,2048,3584]{2,1,0:T(8,128)(2,1)} %all-gather.12.cloned.1.call-done), kind=kOutput, calls=%fused_computation.17 | convolution fusion | flops 3288793088 | bytes 17203200 | tf_op jit(solution)/shard_map/dot_general | solution.py:139
  119.4 17.9 %all-gather.8.cloned.1.call-done = bf16[3584,224]{0,1:T(8,128)(2,1)} async-done(((bf16[896,224]{0,1:T(8,128)(2,1)}), bf16[3584,224]{0,1:T(8,128)(2,1)}) %all-gather.8.cloned.1.call-update) | async-done | bytes 1605648 | tf_op jit(solution)/shard_map/all_gather | solution.py:132
  137.3 9.9 %fusion.19 = bf16[2048,1,224]{0,2,1:T(8,128)(2,1)S(1)} fusion(bf16[3584,224]{0,1:T(8,128)(2,1)} %all-gather.8.cloned.1.call-done, bf16[1,2048,3584]{2,1,0:T(8,128)(2,1)} %all-gather.12.cloned.1.call-done), kind=kOutput, calls=%fused_computation.18 | convolution fusion | flops 3288793088 | bytes 17203200 | tf_op jit(solution)/shard_map/dot_general | solution.py:136
  148.6 6.2 copy.89
  154.8 7.7 %all-to-all-start = ((bf16[2048,2,224]{2,1,0:T(2,128)(2,1)}), bf16[2048,2,224]{2,1,0:T(2,128)(2,1)}, u32[]{:S(2)}, u32[]{:S(2)}) async-start(bf16[2048,2,224]{2,1,0:T(2,128)(2,1)} %copy.89), calls=%async_computation | async-start | bytes 4194304 | tf_op jit(solution)/shard_map/all_to_all | solution.py:82
  163.7 27.2 %all-to-all-done = bf16[2048,2,224]{2,1,0:T(2,128)(2,1)} async-done(((bf16[2048,2,224]{2,1,0:T(2,128)(2,1)}), bf16[2048,2,224]{2,1,0:T(2,128)(2,1)}, u32[]{:S(2)}, u32[]{:S(2)}) %all-to-all-start) | async-done | bytes 1835040 | tf_op jit(solution)/shard_map/all_to_all | solution.py:82
  213.4 6.0 fusion.8
  220.3 23.7 %all-gather.2 = f32[32,1,112]{2,1,0:T(1,128)S(1)} all-gather(f32[1,1,112]{2,1,0:T(1,128)S(1)} %get-tuple-element.141), channel_id=1, replica_groups=mesh['req'=4,'seq'=32] {'seq'}, dimensions={0}, use_global_device_ids=true | all-gather | bytes 14784 | tf_op jit(solution)/shard_map/all_gather | solution.py:21
  255.8 295.2 %all-gather.14.cloned.1.call-done = f32[3584,64,64]{2,1,0:T(8,128)} async-done(((f32[112,64,64]{2,1,0:T(8,128)}), f32[3584,64,64]{2,1,0:T(8,128)}) %all-gather.14.cloned.1.call-update) | async-done | bytes 58720272 | tf_op jit(solution)/shard_map/all_gather | solution.py:21
  551.0 179.3 %while.14 = (s32[]{:T(128)}, f32[112,64,64]{2,1,0:T(8,128)}, s32[]{:T(128)}, f32[32,112]{1,0:T(8,128)S(1)}, f32[32,112,64,64]{3,2,1,0:T(8,128)}, /*index=5*/s32[]{:T(128)}, s32[]{:T(128)}) while((s32[]{:T(128)}, f32[112,64,64]{2,1,0:T(8,128)}, s32[]{:T(128)}, f32[32,112]{1,0:T(8,128)S(1)}, f32[32,112,64,64]{3,2,1,0:T(8,128)}, ...), condition=%wide.region_2.3_spmd.clone, body=%wide.region_1.2_spmd.clone.sunk | while | flops 1835012 | bytes 5506481 | solution.py:33
  555.5 5.6 fusion.58
  566.8 5.6 fusion.58
  572.4 5.6 fusion.58
  578.0 5.6 fusion.58
  583.7 5.6 fusion.58
  589.3 5.6 fusion.58
  606.2 5.7 fusion.58
  611.9 5.7 fusion.58
  628.9 5.6 fusion.58
  696.5 5.7 fusion.58
  702.2 5.6 fusion.58
  732.4 10.9 %multiply_reduce_fusion = (f32[64,112]{0,1:T(8,128)S(1)}, f32[64,112,64]{0,2,1:T(8,128)}) fusion(f32[64,112,64]{0,2,1:T(8,128)} %bitcast.121, f32[64,112,64]{0,2,1:T(8,128)} %bitcast.116, f32[112]{0:T(128)S(1)} %copy-done.13, f32[112,64,64]{2,1,0:T(8,128)S(1)} %copy-done.2, f32[64,112,64]{2,0,1:T(8,128)S(1)} %bitcast.120, f32[64,112]{0,1:T(8,128)S(1)} %copy.98, ...), kind=kOutput, calls=%fused_computation.12 | convolution fusion | flops 357360640 | bytes 11067840 | tf_op jit(solution)/shard_map/ihn,hpn->ihp/dot_general | solution.py:61
  (138 shorter events, 169.3 us)
Async XLA Ops:
  6.5 156.7 %copy-start = (bf16[3584,256]{1,0:T(8,128)(2,1)S(1)}, bf16[3584,256]{1,0:T(8,128)(2,1)}, u32[]{:S(2)}) copy-start(bf16[3584,256]{1,0:T(8,128)(2,1)} %param.17) | copy-start | bytes 5505028
  6.5 32.8 %all-gather.10.cloned.1.call-start = ((), (), s32[]{:S(2)}) async-start(), calls=%async_computation.2 | async-start | bytes 2007040 | tf_op jit(solution)/shard_map/all_gather | solution.py:133
  7.3 102.2 %all-gather.12.cloned.1.call-start = ((), (), s32[]{:S(2)}) async-start(), calls=%async_computation.3 | async-start | bytes 15138816 | tf_op jit(solution)/shard_map/all_gather | solution.py:135
  8.0 129.3 %all-gather.8.cloned.1.call-start = ((), (), s32[]{:S(2)}) async-start(), calls=%async_computation.1 | async-start | bytes 2007040 | tf_op jit(solution)/shard_map/all_gather | solution.py:132
  154.8 7.8 %copy-start.6 = (bf16[1,64,3584]{2,1,0:T(8,128)(2,1)S(1)}, bf16[1,64,3584]{2,1,0:T(8,128)(2,1)}, u32[]{:S(2)}) copy-start(bf16[1,64,3584]{2,1,0:T(8,128)(2,1)} %param.14) | copy-start | bytes 1376260
  154.8 7.8 %copy-start.7 = (bf16[3584,112]{0,1:T(8,128)(2,1)S(1)}, bf16[3584,112]{0,1:T(8,128)(2,1)}, u32[]{:S(2)}) copy-start(bf16[3584,112]{0,1:T(8,128)(2,1)} %param.18) | copy-start | bytes 2408452
  154.8 7.8 %copy-start.11 = (f32[112]{0:T(128)S(1)}, f32[112]{0:T(128)}, u32[]{:S(2)}) copy-start(f32[112]{0:T(128)} %param.19) | copy-start | bytes 1348
  154.8 8.3 %copy-start.12 = (f32[112]{0:T(128)S(1)}, f32[112]{0:T(128)}, u32[]{:S(2)}) copy-start(f32[112]{0:T(128)} %param.20) | copy-start | bytes 1348
  154.8 36.1 %all-to-all-start = ((bf16[2048,2,224]{2,1,0:T(2,128)(2,1)}), bf16[2048,2,224]{2,1,0:T(2,128)(2,1)}, u32[]{:S(2)}, u32[]{:S(2)}) async-start(bf16[2048,2,224]{2,1,0:T(2,128)(2,1)} %copy.89), calls=%async_computation | async-start | bytes 4194304 | tf_op jit(solution)/shard_map/all_to_all | solution.py:82
  162.6 388.4 %all-gather.14.cloned.1.call-start = ((), (), s32[]{:S(2)}) async-start(), calls=%async_computation.4 | async-start | bytes 121110528 | tf_op jit(solution)/shard_map/all_gather | solution.py:21
  199.6 1.8 copy-start.4
  199.7 4.2 copy-start.8
  201.5 3.7 copy-start.9
  201.5 3.4 collective-permute-start
  211.3 2.0 copy-start.3
  249.4 1.5 copy-start.5
  730.3 2.0 copy-start.2
  730.3 2.0 copy-start.13
  746.7 3.7 copy-start.10
  746.7 7.6 copy-start.1
Sparse Core Ops, SparseCore 0:
  9.0 30.2 all-gather.9
  41.6 67.8 all-gather.11
  111.1 26.1 all-gather.7
  219.5 331.4 all-gather.13
where the time goes:
time: 761 us
  waiting for transfers between devices  444 us (58%)
  other arithmetic  189 us (25%)
  matrix products  42.6 us (6%)
  local copies, waits for them, and re-layouts  37.7 us (5%)
  blocking collectives  23.7 us (3%)
  between operations  14.1 us (2%)
  starting transfers between devices  10.2 us (1%)
    all_gather x1, waiting for transfers between devices, prefix(): everything = jax.tree.map(lambda part: lax.all_gather(part, axis), shard)  295 us
    select_n x32, other arithmetic, hop(): return jax.tree.map(lambda a, b: jnp.where(reached, a, b), new, before)  179 us
    all_gather x1, waiting for transfers between devices, local(): shard_piece = lax.all_gather(own_rows, 'seq', axis=0, tiled=True)  70.1 us
    all_gather x1, waiting for transfers between devices, local(): lax.all_gather(w_x, 'req', axis=0, tiled=True)  30.6 us
    all_to_all x1, waiting for transfers between devices, position_mix(): lax.all_to_all(stacked, 'seq', split_axis=0, concat_axis=2, tiled=True)  27.2 us
    all_gather x1, blocking collectives, prefix(): everything = jax.tree.map(lambda part: lax.all_gather(part, axis), shard)  23.7 us
    all_gather x1, waiting for transfers between devices, local(): lax.all_gather(w_z, 'req', axis=0, tiled=True)  17.9 us
  transfers between devices with their start and end apart: 6, of which 6 were waited for; matrix products, arithmetic and copies ran while one was open for 3% of the time, Pallas kernels for 0%

commit v1 on v0

v1 whole, which is shorter than its diff:
```python
import functools

import jax
import jax.numpy as jnp
from jax import lax
from jax.experimental import pallas as pl
from jax.experimental.pallas import tpu as pltpu
from jax.sharding import PartitionSpec as P

GROUPS = 2
STATE = 64
HEAD = 64
TILE = 128
SLOT = 256
PIECES = 4


def split(value):
    high = value.astype(jnp.bfloat16)
    return high, (value - high.astype(jnp.float32)).astype(jnp.bfloat16)


def matmul(a, b, dims=((1,), (0,))):
    return lax.dot_general(a, b, (dims, ((), ())), preferred_element_type=jnp.float32)


def scan_kernel(*refs):
    projected = refs[:PIECES]
    taps, conv_bias, head_rows, skip, out, xbc, state = refs[PIECES:]
    step = pl.program_id(0)
    rows = projected[0].shape[1]
    own = rows * PIECES
    past = xbc.shape[0] - TILE

    @pl.when(step == 0)
    def _():
        xbc[...] = jnp.zeros_like(xbc)
        state[...] = jnp.zeros_like(state)

    @pl.when(step > 0)
    def _():
        xbc[0:past] = xbc[TILE : TILE + past]

    gates = []
    for owner in range(TILE // own):
        for piece in range(PIECES):
            block = projected[piece][owner]
            start = past + owner * own + piece * rows
            xbc[start : start + rows, :SLOT] = block[:, :SLOT].astype(jnp.float32)
            xbc[start : start + rows, SLOT:] = block[:, 2 * SLOT :].astype(jnp.float32)
            gates.append(block[:, SLOT : 2 * SLOT])
    gate = jnp.concatenate(gates, axis=0).astype(jnp.float32)

    total = conv_bias[...]
    count = taps.shape[0]
    for k in range(count):
        first = past - (count - 1) + k
        total = total + taps[k : k + 1] * xbc[first : first + TILE]
    conved = (total * jax.nn.sigmoid(total)).astype(jnp.bfloat16)
    b_proj = conved[:, SLOT : SLOT + TILE]
    c_proj = conved[:, SLOT + TILE :]

    raw = xbc[past : past + TILE, SLOT + TILE :]
    step_size = jax.nn.softplus(raw + head_rows[0:1])
    log_decay = -step_size * head_rows[1:2]
    row = lax.broadcasted_iota(jnp.int32, (TILE, TILE), 0)
    lane = lax.broadcasted_iota(jnp.int32, (TILE, TILE), 1)
    causal = row >= lane
    running = jnp.dot(
        causal.astype(jnp.float32),
        log_decay,
        precision=lax.Precision.HIGHEST,
        preferred_element_type=jnp.float32,
    )
    running_rows = running.T
    step_rows = step_size.T
    affinity = jnp.where(causal, matmul(c_proj, b_proj, ((1,), (1,))), 0.0)
    before = state[...]
    before_high, before_low = split(before)
    carried = matmul(c_proj, before_high) + matmul(c_proj, before_low)

    left = lane < HEAD
    for tile in range(SLOT // TILE):
        span = slice(tile * TILE, (tile + 1) * TILE)
        x = conved[:, span]
        mixing, columns, steps = [], [], []
        for half in range(2):
            at = STATE + 2 * tile + half
            column = jnp.broadcast_to(running[:, at : at + 1], (TILE, TILE))
            decay = jnp.exp(jnp.minimum(column - running_rows[at : at + 1], 0.0))
            mixing.append(decay * affinity * step_rows[at : at + 1])
            columns.append(column)
            steps.append(jnp.broadcast_to(step_size[:, at : at + 1], (TILE, TILE)))
        weights, rest = split(jnp.concatenate(mixing, axis=1))
        zero = jnp.zeros_like(x)
        values = jnp.concatenate([jnp.where(left, x, zero), jnp.where(left, zero, x)], axis=0)
        intra = matmul(weights, values) + matmul(rest, values)
        run = jnp.where(left, columns[0], columns[1])
        last = run[TILE - 1 :]
        x32 = x.astype(jnp.float32)
        result = intra + jnp.exp(run) * carried[:, span] + skip[:, span] * x32
        z = gate[:, span]
        gated = (result * (z * jax.nn.sigmoid(z))).astype(jnp.bfloat16)
        width = min(out.shape[2] - tile * TILE, TILE)
        for owner in range(TILE // own):
            out[owner, :, tile * TILE : tile * TILE + width] = gated[
                owner * own : (owner + 1) * own, :width
            ]
        added = x32 * (jnp.exp(last - run) * jnp.where(left, steps[0], steps[1]))
        added_high, added_low = split(added)
        block = matmul(b_proj, added_high, ((0,), (0,))) + matmul(b_proj, added_low, ((0,), (0,)))
        state[:, span] = jnp.exp(last) * before[:, span] + block


def scan(projected, taps, conv_bias, head_rows, skip, width):
    owners, rows, columns = projected[0].shape
    own = rows * PIECES
    per_step = TILE // own
    whole = lambda array: pl.BlockSpec(array.shape, lambda i: (0,) * array.ndim)
    constants = (taps, conv_bias, head_rows, skip)
    return pl.pallas_call(
        scan_kernel,
        grid=(owners // per_step,),
        in_specs=[pl.BlockSpec((per_step, rows, columns), lambda i: (i, 0, 0))] * PIECES
        + [whole(array) for array in constants],
        out_specs=pl.BlockSpec((per_step, own, width), lambda i: (i, 0, 0)),
        out_shape=jax.ShapeDtypeStruct((owners, own, width), jnp.bfloat16),
        scratch_shapes=[
            pltpu.VMEM((TILE + 8, 2 * SLOT), jnp.float32),
            pltpu.VMEM((TILE, SLOT), jnp.float32),
        ],
        name="mixer_scan",
    )(*projected, *constants)


def norm_kernel(turned, limit, gated, gain, out):
    owners, rows, width = gated.shape
    per_group = owners // GROUPS
    position = lax.broadcasted_iota(jnp.int32, (rows, 1), 0)
    valid = position < limit[0]
    for group in range(GROUPS):
        members = range(group * per_group, (group + 1) * per_group)
        squares = jnp.zeros((rows, width), jnp.float32)
        for owner in members:
            block = gated[owner].astype(jnp.float32)
            squares = squares + block * block
        mean = jnp.sum(squares, axis=1, keepdims=True) * (1.0 / (per_group * width))
        scale = jnp.where(valid, lax.rsqrt(mean + 1e-05), 0.0)
        for owner in members:
            block = gated[owner].astype(jnp.float32) * scale * gain[owner : owner + 1]
            block = jnp.where(valid, block, 0.0).astype(jnp.bfloat16)
            start = owner * width
            if owner % 2 == 0:
                out[:, start : start + width] = block
            else:
                out[:, start + turned : start + width] = block[:, : width - turned]
                out[:, start : start + turned] = block[:, width - turned :]


def norm(limit, gated, gain, turned):
    owners, rows, width = gated.shape
    return pl.pallas_call(
        functools.partial(norm_kernel, turned),
        in_specs=[
            pl.BlockSpec(memory_space=pltpu.SMEM),
            pl.BlockSpec(memory_space=pltpu.VMEM),
            pl.BlockSpec(memory_space=pltpu.VMEM),
        ],
        out_specs=pl.BlockSpec(memory_space=pltpu.VMEM),
        out_shape=jax.ShapeDtypeStruct((rows, owners * width), jnp.bfloat16),
        name="gated_norm",
    )(limit, gated, gain)


def around(block, axis, distance):
    size = lax.axis_size(axis)
    return lax.ppermute(block, axis, [(i, (i + distance) % size) for i in range(size)])


def gather_rows(block, axis):
    depth = block.shape[0]
    half = depth // 2
    behind, ahead = around(block, axis, 1), around(block, axis, -1)
    far = jnp.concatenate(
        [around(behind[:half], axis, 1), around(ahead[half:], axis, -1)], axis=0
    )
    me = lax.axis_index(axis)
    whole = jnp.zeros((4 * depth,) + block.shape[1:], block.dtype)
    for distance, part in ((0, block), (3, behind), (1, ahead), (2, far)):
        whole = lax.dynamic_update_slice(whole, part, ((me + distance) % 4 * depth, 0))
    return whole


def local(
    tokens,
    w_z,
    w_x,
    w_bc,
    w_dt,
    dt_bias,
    a_rate,
    conv_weight,
    conv_bias,
    d_skip,
    norm_gain,
    lengths,
):
    own_rows = tokens[0]
    num_rows, depth = own_rows.shape
    width = w_x.shape[1]
    me = lax.axis_index("seq")
    owners = lax.axis_size("seq")
    odd = me % 2 == 1
    chip_heads = 2 * width // HEAD
    turned = width - 3 * HEAD
    inner = norm_gain.shape[0]
    group = me // (owners // GROUPS)

    rows = num_rows // PIECES
    token_pieces = [
        lax.all_gather(own_rows[j * rows : (j + 1) * rows], "seq") for j in range(PIECES)
    ]

    def turn(columns):
        return jnp.where(odd, jnp.roll(columns, -turned, axis=-1), columns)

    def pad(array, size):
        return jnp.pad(array, ((0, 0), (0, size - array.shape[-1])))

    def heads_of(array):
        chip = lax.dynamic_slice_in_dim(array, me // 2 * chip_heads, chip_heads, -1)
        return jnp.where(
            odd, jnp.concatenate([chip[..., 4:7], chip[..., 3:4]], axis=-1), chip[..., :4]
        )

    def states_of(array, start):
        first = lax.dynamic_slice_in_dim(array, start + group * STATE, STATE, -1)
        second = lax.dynamic_slice_in_dim(
            array, start + (GROUPS + group) * STATE, STATE, -1
        )
        return first, second

    both = gather_rows(jnp.concatenate([turn(w_x), turn(w_z)], axis=1), "req")
    w_b, w_c = states_of(w_bc, 0)
    weights = jnp.concatenate(
        [
            pad(both[:, :width], SLOT),
            pad(both[:, width:], SLOT),
            pad(w_b, TILE),
            pad(jnp.concatenate([w_c, heads_of(w_dt)], axis=1), TILE),
        ],
        axis=1,
    )

    def channels_of(array):
        x_part = turn(lax.dynamic_slice_in_dim(array, me * width, width, -1))
        b_part, c_part = states_of(array, inner)
        return jnp.concatenate([pad(x_part, SLOT), pad(b_part, TILE), pad(c_part, TILE)], axis=1)

    taps = channels_of(conv_weight)
    bias = channels_of(conv_bias[None])
    head_rows = jnp.pad(
        jnp.stack([heads_of(dt_bias), heads_of(a_rate)]), ((0, 0), (STATE, TILE - STATE - 4))
    )
    skip = jnp.repeat(heads_of(d_skip), HEAD)[None]
    gains = norm_gain.reshape(owners, width)
    gains = jnp.where(
        (jnp.arange(owners) % 2 == 1)[:, None], jnp.roll(gains, -turned, axis=1), gains
    )

    projected = []
    for piece in token_pieces:
        block = jnp.dot(
            piece.reshape(owners * rows, depth), weights, preferred_element_type=jnp.float32
        ).astype(jnp.bfloat16)
        projected.append(block.reshape(owners, rows, -1))
    gated = scan(projected, taps, bias, head_rows, skip, width)
    mine = lax.all_to_all(gated, "seq", split_axis=0, concat_axis=0, tiled=True)
    limit = lengths - me * num_rows
    return norm(limit, mine, gains, turned)[None]


def solution(mesh):
    placed = (
        P("req", "seq", None),
        P("req", "seq"),
        P("req", "seq"),
        P(),
        P(),
        P(),
        P(),
        P(),
        P(),
        P(),
        P(),
        P("req"),
    )
    return jax.shard_map(
        local, mesh=mesh, in_specs=placed, out_specs=P("req", "seq", None), check_vma=False
    )
```

time: 761 us -> 258 us (0.34)
  waiting for transfers between devices: 444 us -> 134 us
  other arithmetic: 189 us -> 14.4 us
  blocking collectives: 23.7 us -> 0 us
  Pallas kernels: 0 us -> 18.2 us
  matrix products: 42.6 us -> 30.4 us
    all_gather x4, waiting for transfers between devices: 414 us -> 117 us  [local(): lax.all_gather(own_rows[j * rows:(j + 1) * rows], 'seq')]
    select_n x32 -> x6, other arithmetic: 179 us -> 4.22 us  [the longest x3 1.83 us: turn(): return jnp.where(odd, jnp.roll(columns, -turned, axis=-1), columns)]
    all_gather x1 -> x0, blocking collectives: 23.7 us -> none  [prefix(): everything = jax.tree.map(lambda part: lax.all_gather(part, axis), shard)]
    pallas_call x0 -> x2, Pallas kernels: none -> 18.2 us  [the longest x1 15.5 us: scan(): pl.pallas_call(scan_kernel, grid=(owners // per_step,), in_specs=[pl.Bloc...]
    dot_general x8 -> x4, matrix products: 42.6 us -> 30.4 us  [local(): jnp.dot(piece.reshape(owners * rows, depth), weights, preferred_element_t...]
    all_to_all x1, waiting for transfers between devices: 27.2 us -> 15.4 us  [local(): mine = lax.all_to_all(gated, 'seq', split_axis=0, concat_axis=0, tiled=True)]
    all_to_all x3 -> x0, local copies, waits for them, and re-layouts: 8.73 us -> none  [position_mix(): lax.all_to_all(stacked, 'seq', split_axis=0, concat_axis=2, tiled=True)]
    slice x7 -> x21, local copies, waits for them, and re-layouts: 6.86 us -> 15.1 us  [the longest x7 5.27 us: turn(): return jnp.where(odd, jnp.roll(columns, -turned, axis=-1), columns)]
  transfers between devices with their start and end apart: 6 -> 9, of which waited for: 6 -> 4; matrix products, arithmetic and copies ran while one was open for 3% -> 26% of each run, Pallas kernels for 0% -> 0%
where the time goes in v1:
time: 258 us; the launch traced here: 256 us
  waiting for transfers between devices  134 us (52%)
  local copies, waits for them, and re-layouts  32 us (12%)
  matrix products  30.4 us (12%)
  Pallas kernels  18.2 us (7%)
  other arithmetic  14.4 us (6%)
  between operations  14 us (5%)
  starting transfers between devices  12.7 us (5%)
    all_gather x4, waiting for transfers between devices, local(): lax.all_gather(own_rows[j * rows:(j + 1) * rows], 'seq')  117 us
    dot_general x4, matrix products, local(): jnp.dot(piece.reshape(owners * rows, depth), weights, preferred_element_t...  30.4 us
    pallas_call x1, Pallas kernels, scan(): pl.pallas_call(scan_kernel, grid=(owners // per_step,), in_specs=[pl.Bloc...  15.5 us
    all_to_all x1, waiting for transfers between devices, local(): mine = lax.all_to_all(gated, 'seq', split_axis=0, concat_axis=0, tiled=True)  15.4 us
    ppermute x4, starting transfers between devices, around(): lax.ppermute(block, axis, [(i, (i + distance) % size) for i in range(size)])  7.27 us
    unnamed x20, local copies, waits for them, and re-layouts  6.45 us
    all_to_all x1, starting transfers between devices, local(): mine = lax.all_to_all(gated, 'seq', split_axis=0, concat_axis=0, tiled=True)  5.28 us
    slice x7, local copies, waits for them, and re-layouts, turn(): return jnp.where(odd, jnp.roll(columns, -turned, axis=-1), columns)  5.27 us
  transfers between devices with their start and end apart: 9, of which 4 were waited for; matrix products, arithmetic and copies ran while one was open for 26% of the time, Pallas kernels for 0%

profile of v1, /device:TPU:1, one launch (start us, length us, event | category | flops | bytes accessed | tf_op | source)
XLA Modules:
  0.0 255.7 jit_solution(17750527511384385169)
XLA Ops:
  6.5 1.9 fusion.14
  15.1 2.5 collective-permute-start
  17.6 2.1 collective-permute-start.1
  32.6 2.9 %constant_dynamic-slice_fusion.7 = (bf16[3584,64]{1,0:T(8,128)(2,1)}, bf16[3584,64]{1,0:T(8,128)(2,1)S(1)}) fusion(bf16[3584,256]{1,0:T(8,128)(2,1)} %param.15, s32[]{:T(128)S(6)} %select_n.151, s32[]{:T(128)S(6)} %select_n.152), kind=kLoop, calls=%fused_computation.43 | loop fusion | bytes 1835016 | tf_op jit(solution)/shard_map/dynamic_slice | solution.py:237
  36.1 1.3 fusion.11
  37.4 1.4 pad_maximum_fusion
  38.9 1.8 slice.133
  40.7 2.0 slice.134
  42.7 2.7 %collective-permute-start.3 = (bf16[448,448]{0,1:T(8,128)(2,1)}, bf16[448,448]{0,1:T(8,128)(2,1)}, u32[]{:S(2)}, u32[]{:S(2)}) collective-permute-start(bf16[448,448]{0,1:T(8,128)(2,1)} %slice.134), channel_id=1, source_target_pairs={{0,96},{32,0},{64,32},{96,64},{1,97},{33,1},{65,33},{97,65},{2,98}... | collective-permute-start | bytes 1204232 | tf_op jit(solution)/shard_map/ppermute | solution.py:177
  46.0 2.3 copy.20
  48.4 2.3 copy.19
  54.6 1.4 maximum_dynamic-update-slice_fusion
  57.2 3.0 %fusion.6 = bf16[3584,768]{0,1:T(8,128)(2,1)} fusion(bf16[3584,68]{0,1:T(8,128)(2,1)S(1)} %copy-done.2, bf16[3584,64]{0,1:T(8,128)(2,1)S(1)} %copy-done.3, bf16[3584,224]{0,1:T(8,128)(2,1)S(1)} %slice.136, bf16[3584,256]{0,1:T(8,128)(2,1)S(1)} %slice_select_fusion), kind=kLoop, calls=%fused_computation.11 | loop fusion | flops 49545216 | bytes 9891840 | tf_op jit(solution)/shard_map/concatenate | solution.py:245
  60.2 7.6 %convolution_convert_fusion = bf16[768,512]{0,1:T(8,128)(2,1)} fusion(bf16[3584,768]{0,1:T(8,128)(2,1)} %fusion.6, bf16[512,3584]{1,0:T(8,128)(2,1)} %bitcast.47), kind=kOutput, calls=%fused_computation.14 | convolution fusion | flops 2818965504 | bytes 9961472 | tf_op jit(solution)/shard_map/dot_general | solution.py:273
  67.8 38.1 %all-gather.5.cloned.1.call-done = bf16[32,16,3584]{2,1,0:T(8,128)(2,1)} async-done(((bf16[1,16,3584]{2,1,0:T(8,128)(2,1)}), bf16[32,16,3584]{2,1,0:T(8,128)(2,1)}) %all-gather.5.cloned.1.call-update) | async-done | bytes 3670032 | tf_op jit(solution)/shard_map/all_gather | solution.py:221
  105.9 7.6 %convolution_convert_fusion.3 = bf16[768,512]{0,1:T(8,128)(2,1)} fusion(bf16[3584,768]{0,1:T(8,128)(2,1)} %fusion.6, bf16[512,3584]{1,0:T(8,128)(2,1)} %bitcast.48), kind=kOutput, calls=%fused_computation.17 | convolution fusion | flops 2818965504 | bytes 9961472 | tf_op jit(solution)/shard_map/dot_general | solution.py:273
  113.5 39.6 %all-gather.7.cloned.1.call-done = bf16[32,16,3584]{2,1,0:T(8,128)(2,1)} async-done(((bf16[1,16,3584]{2,1,0:T(8,128)(2,1)}), bf16[32,16,3584]{2,1,0:T(8,128)(2,1)}) %all-gather.7.cloned.1.call-update) | async-done | bytes 3670032 | tf_op jit(solution)/shard_map/all_gather | solution.py:221
  153.1 7.6 %convolution_convert_fusion.2 = bf16[768,512]{0,1:T(8,128)(2,1)} fusion(bf16[3584,768]{0,1:T(8,128)(2,1)} %fusion.6, bf16[512,3584]{1,0:T(8,128)(2,1)} %bitcast.49), kind=kOutput, calls=%fused_computation.16 | convolution fusion | flops 2818965504 | bytes 9961472 | tf_op jit(solution)/shard_map/dot_general | solution.py:273
  160.7 39.4 %all-gather.9.cloned.1.call-done = bf16[32,16,3584]{2,1,0:T(8,128)(2,1)} async-done(((bf16[1,16,3584]{2,1,0:T(8,128)(2,1)}), bf16[32,16,3584]{2,1,0:T(8,128)(2,1)}) %all-gather.9.cloned.1.call-update) | async-done | bytes 3670032 | tf_op jit(solution)/shard_map/all_gather | solution.py:221
  200.1 7.6 %convolution_convert_fusion.1 = bf16[768,512]{0,1:T(8,128)(2,1)} fusion(bf16[3584,768]{0,1:T(8,128)(2,1)} %fusion.6, bf16[512,3584]{1,0:T(8,128)(2,1)} %bitcast.50), kind=kOutput, calls=%fused_computation.15 | convolution fusion | flops 2818965504 | bytes 9961472 | tf_op jit(solution)/shard_map/dot_general | solution.py:273
  207.7 15.5 %mixer_scan.1 = bf16[32,64,224]{2,1,0:T(8,128)(2,1)} custom-call(bf16[32,16,768]{2,1,0:T(8,128)(2,1)} %bitcast.40, bf16[32,16,768]{2,1,0:T(8,128)(2,1)} %bitcast.41, bf16[32,16,768]{2,1,0:T(8,128)(2,1)} %bitcast.42, bf16[32,16,768]{2,1,0:T(8,128)(2,1)} %bitcast.39, f32[4,512]{1,0:T(4,128)} %select_maximum_fusion.refs_4_, f32[1,512]{1,0:T(1,128)} %fusion.10.refs_5_, ...), custom_call_target="tpu_custom_call" | custom-call | tf_op jit(solution)/shard_map/mixer_scan/pallas_call | solution.py:121
  223.2 5.3 %all-to-all-start = ((bf16[32,64,224]{2,1,0:T(8,128)(2,1)}), bf16[32,64,224]{2,1,0:T(8,128)(2,1)S(1)}, u32[]{:S(2)}, u32[]{:S(2)}) async-start(bf16[32,64,224]{2,1,0:T(8,128)(2,1)} %mixer_scan.1), calls=%async_computation | async-start | bytes 2097152 | tf_op jit(solution)/shard_map/all_to_all | solution.py:278
  230.0 15.4 %all-to-all-done.gated = bf16[32,64,224]{2,1,0:T(8,128)(2,1)S(1)} async-done(((bf16[32,64,224]{2,1,0:T(8,128)(2,1)}), bf16[32,64,224]{2,1,0:T(8,128)(2,1)S(1)}, u32[]{:S(2)}, u32[]{:S(2)}) %all-to-all-start) | async-done | bytes 917536 | tf_op jit(solution)/shard_map/all_to_all | solution.py:278
  246.4 2.8 %gated_norm.1 = bf16[64,7168]{1,0:T(8,128)(2,1)} custom-call(s32[1]{0:T(128)S(6)} %sub.17.limit, bf16[32,64,224]{2,1,0:T(8,128)(2,1)} %copy-done, f32[32,224]{1,0:T(8,128)} %maximum_select_fusion.2.gain), custom_call_target="tpu_custom_call" | custom-call | tf_op jit(solution)/shard_map/gated_norm/pallas_call | solution.py:162
  (76 shorter events, 27.5 us)
Async XLA Ops:
  6.5 53.7 %all-gather.11.cloned.1.call-start = ((), (), s32[]{:S(2)}) async-start(), calls=%async_computation.4 | async-start | bytes 3784704 | tf_op jit(solution)/shard_map/all_gather | solution.py:221
  8.4 97.5 %all-gather.5.cloned.1.call-start = ((), (), s32[]{:S(2)}) async-start(), calls=%async_computation.1 | async-start | bytes 3784704 | tf_op jit(solution)/shard_map/all_gather | solution.py:221
  9.2 143.9 %all-gather.7.cloned.1.call-start = ((), (), s32[]{:S(2)}) async-start(), calls=%async_computation.2 | async-start | bytes 3784704 | tf_op jit(solution)/shard_map/all_gather | solution.py:221
  9.9 190.2 %all-gather.9.cloned.1.call-start = ((), (), s32[]{:S(2)}) async-start(), calls=%async_computation.3 | async-start | bytes 3784704 | tf_op jit(solution)/shard_map/all_gather | solution.py:221
  13.7 9.4 %copy-start.6 = (f32[112]{0:T(128)S(1)}, f32[112]{0:T(128)}, u32[]{:S(2)}) copy-start(f32[112]{0:T(128)} %param.17) | copy-start | bytes 1348
  13.7 10.1 %copy-start.7 = (f32[112]{0:T(128)S(1)}, f32[112]{0:T(128)}, u32[]{:S(2)}) copy-start(f32[112]{0:T(128)} %param.18) | copy-start | bytes 1348
  13.7 10.9 %copy-start.8 = (f32[112]{0:T(128)S(1)}, f32[112]{0:T(128)}, u32[]{:S(2)}) copy-start(f32[112]{0:T(128)} %param.21) | copy-start | bytes 1348
  15.1 23.7 %collective-permute-start = (bf16[896,448]{0,1:T(8,128)(2,1)}, bf16[896,448]{0,1:T(8,128)(2,1)}, u32[]{:S(2)}, u32[]{:S(2)}) collective-permute-start(bf16[896,448]{0,1:T(8,128)(2,1)} %get-tuple-element.7), channel_id=1, source_target_pairs={{0,32},{32,64},{64,96},{96,0},{1,33},{33,65},{65,97},{97,1},{2,34}... | collective-permute-start | bytes 2408456 | tf_op jit(solution)/shard_map/ppermute | solution.py:177
  17.6 23.1 %collective-permute-start.1 = (bf16[896,448]{0,1:T(8,128)(2,1)}, bf16[896,448]{0,1:T(8,128)(2,1)}, u32[]{:S(2)}, u32[]{:S(2)}) collective-permute-start(bf16[896,448]{0,1:T(8,128)(2,1)} %get-tuple-element.7), channel_id=1, source_target_pairs={{0,96},{32,0},{64,32},{96,64},{1,97},{33,1},{65,33},{97,65},{2,98}... | collective-permute-start | bytes 2408456 | tf_op jit(solution)/shard_map/ppermute | solution.py:177
  30.2 7.2 %copy-start.1 = (bf16[3584,4]{1,0:T(8,128)(2,1)S(1)}, bf16[3584,4]{1,0:T(8,128)(2,1)}, u32[]{:S(2)}) copy-start(bf16[3584,4]{1,0:T(8,128)(2,1)} %copy.16) | copy-start | bytes 86020
  40.7 13.9 %collective-permute-start.2 = (bf16[448,448]{0,1:T(8,128)(2,1)}, bf16[448,448]{0,1:T(8,128)(2,1)}, u32[]{:S(2)}, u32[]{:S(2)}) collective-permute-start(bf16[448,448]{0,1:T(8,128)(2,1)} %slice.133), channel_id=1, source_target_pairs={{0,32},{32,64},{64,96},{96,0},{1,33},{33,65},{65,97},{97,1},{2,34}... | collective-permute-start | bytes 1204232 | tf_op jit(solution)/shard_map/ppermute | solution.py:177
  42.7 11.8 %collective-permute-start.3 = (bf16[448,448]{0,1:T(8,128)(2,1)}, bf16[448,448]{0,1:T(8,128)(2,1)}, u32[]{:S(2)}, u32[]{:S(2)}) collective-permute-start(bf16[448,448]{0,1:T(8,128)(2,1)} %slice.134), channel_id=1, source_target_pairs={{0,96},{32,0},{64,32},{96,64},{1,97},{33,1},{65,33},{97,65},{2,98}... | collective-permute-start | bytes 1204232 | tf_op jit(solution)/shard_map/ppermute | solution.py:177
  53.3 2.9 %copy-start.5 = (pred[256]{0:T(512)(128)(4,1)S(1)}, pred[256]{0:T(512)(128)(4,1)}, u32[]{:S(2)}) copy-start(pred[256]{0:T(512)(128)(4,1)} %constant.91.clone.1) | copy-start | bytes 772
  56.0 1.0 copy-start.2
  56.1 1.2 copy-start.3
  207.7 20.8 %copy-start.4 = (f32[7168]{0:T(1024)S(1)}, f32[7168]{0:T(1024)}, u32[]{:S(2)}) copy-start(f32[7168]{0:T(1024)} %param.22) | copy-start | bytes 86020
  223.2 22.2 %all-to-all-start = ((bf16[32,64,224]{2,1,0:T(8,128)(2,1)}), bf16[32,64,224]{2,1,0:T(8,128)(2,1)S(1)}, u32[]{:S(2)}, u32[]{:S(2)}) async-start(bf16[32,64,224]{2,1,0:T(8,128)(2,1)} %mixer_scan.1), calls=%async_computation | async-start | bytes 2097152 | tf_op jit(solution)/shard_map/all_to_all | solution.py:278
  245.4 1.0 copy-start
Sparse Core Ops, SparseCore 0:
  9.6 49.1 all-gather.10
  61.1 44.7 all-gather.4
  108.2 44.8 all-gather.6
  155.2 44.8 all-gather.8

commit v2 on v1

--- a/solution.py
+++ b/solution.py
@@ -12,7 +12,7 @@
 HEAD = 64
 TILE = 128
 SLOT = 256
-PIECES = 4
+PIECES = 1
 
 
 def split(value):

time: 258 us -> 155 us (0.60)
  waiting for transfers between devices: 134 us -> 41 us
  matrix products: 30.4 us -> 21.4 us
    all_gather x4 -> x1, waiting for transfers between devices: 117 us -> 24.8 us  [local(): lax.all_gather(own_rows[j * rows:(j + 1) * rows], 'seq')]
    dot_general x4 -> x1, matrix products: 30.4 us -> 21.4 us  [local(): jnp.dot(piece.reshape(owners * rows, depth), weights, preferred_element_t...]
    concatenate x1 -> x0, other arithmetic: 2.97 us -> none  [local(): jnp.concatenate([pad(both[:, :width], SLOT), pad(both[:, width:], SLOT),...]
    convert_element_type x0 -> x1, local copies, waits for them, and re-layouts: none -> 2.83 us  [local(): block = jnp.dot(piece.reshape(owners * rows, depth), weights, preferred_e...]
    unnamed x20 -> x16, local copies, waits for them, and re-layouts: 6.45 us -> 5.87 us
  transfers between devices with their start and end apart: 9 -> 6, of which waited for: 4 -> 2; matrix products, arithmetic and copies ran while one was open for 26% -> 27% of each run, Pallas kernels for 0% -> 0%
where the time goes in v2:
time: 155 us; the launch traced here: 154 us
  waiting for transfers between devices  41 us (26%)
  local copies, waits for them, and re-layouts  33.5 us (22%)
  matrix products  21.4 us (14%)
  Pallas kernels  18.5 us (12%)
  between operations  14.2 us (9%)
  starting transfers between devices  12.7 us (8%)
  other arithmetic  12.6 us (8%)
    all_gather x1, waiting for transfers between devices, local(): lax.all_gather(own_rows[j * rows:(j + 1) * rows], 'seq')  24.8 us
    dot_general x1, matrix products, local(): jnp.dot(piece.reshape(owners * rows, depth), weights, preferred_element_t...  21.4 us
    pallas_call x1, Pallas kernels, scan(): pl.pallas_call(scan_kernel, grid=(owners // per_step,), in_specs=[pl.Bloc...  15.7 us
    all_to_all x1, waiting for transfers between devices, local(): mine = lax.all_to_all(gated, 'seq', split_axis=0, concat_axis=0, tiled=True)  15.4 us
    ppermute x4, starting transfers between devices, around(): lax.ppermute(block, axis, [(i, (i + distance) % size) for i in range(size)])  7.27 us
    unnamed x16, local copies, waits for them, and re-layouts  5.87 us
    all_to_all x1, starting transfers between devices, local(): mine = lax.all_to_all(gated, 'seq', split_axis=0, concat_axis=0, tiled=True)  5.4 us
    slice x7, local copies, waits for them, and re-layouts, turn(): return jnp.where(odd, jnp.roll(columns, -turned, axis=-1), columns)  5.26 us
  transfers between devices with their start and end apart: 6, of which 2 were waited for; matrix products, arithmetic and copies ran while one was open for 27% of the time, Pallas kernels for 0%

profile of v2, /device:TPU:1, one launch (start us, length us, event | category | flops | bytes accessed | tf_op | source)
XLA Modules:
  0.0 153.7 jit_solution(3146361155098365982)
XLA Ops:
  11.4 1.0 pad_maximum_fusion.1
  12.4 2.5 %collective-permute-start = (bf16[896,448]{0,1:T(8,128)(2,1)}, bf16[896,448]{0,1:T(8,128)(2,1)}, u32[]{:S(2)}, u32[]{:S(2)}) collective-permute-start(bf16[896,448]{0,1:T(8,128)(2,1)} %get-tuple-element.7), channel_id=1, source_target_pairs={{0,32},{32,64},{64,96},{96,0},{1,33},{33,65},{65,97},{97,1},{2,34}... | collective-permute-start | bytes 2408456 | tf_op jit(solution)/shard_map/ppermute | solution.py:177
  14.9 2.1 %collective-permute-start.1 = (bf16[896,448]{0,1:T(8,128)(2,1)}, bf16[896,448]{0,1:T(8,128)(2,1)}, u32[]{:S(2)}, u32[]{:S(2)}) collective-permute-start(bf16[896,448]{0,1:T(8,128)(2,1)} %get-tuple-element.7), channel_id=1, source_target_pairs={{0,96},{32,0},{64,32},{96,64},{1,97},{33,1},{65,33},{97,65},{2,98}... | collective-permute-start | bytes 2408456 | tf_op jit(solution)/shard_map/ppermute | solution.py:177
  22.1 1.3 copy.17
  29.6 3.0 %constant_dynamic-slice_fusion.7 = (bf16[3584,64]{1,0:T(8,128)(2,1)}, bf16[3584,64]{1,0:T(8,128)(2,1)S(1)}) fusion(bf16[3584,256]{1,0:T(8,128)(2,1)} %param.15, s32[]{:T(128)S(6)} %select_n.151, s32[]{:T(128)S(6)} %select_n.152), kind=kLoop, calls=%fused_computation.50 | loop fusion | bytes 1835016 | tf_op jit(solution)/shard_map/dynamic_slice | solution.py:237
  33.2 1.3 fusion.29
  34.5 1.4 pad_maximum_fusion
  35.9 1.8 %slice.113 = bf16[448,448]{0,1:T(8,128)(2,1)} slice(bf16[896,448]{0,1:T(8,128)(2,1)} %collective-permute-done), slice={[0:448], [0:448]} | slice | bytes 802816 | tf_op jit(solution)/shard_map/slice | solution.py:185
  37.8 2.0 %slice.114 = bf16[448,448]{0,1:T(8,128)(2,1)} slice(bf16[896,448]{0,1:T(8,128)(2,1)} %collective-permute-done.1), slice={[448:896], [0:448]} | slice | bytes 802816 | tf_op jit(solution)/shard_map/slice | solution.py:185
  39.8 2.7 %collective-permute-start.3 = (bf16[448,448]{0,1:T(8,128)(2,1)}, bf16[448,448]{0,1:T(8,128)(2,1)}, u32[]{:S(2)}, u32[]{:S(2)}) collective-permute-start(bf16[448,448]{0,1:T(8,128)(2,1)} %slice.114), channel_id=1, source_target_pairs={{0,96},{32,0},{64,32},{96,64},{1,97},{33,1},{65,33},{97,65},{2,98}... | collective-permute-start | bytes 1204232 | tf_op jit(solution)/shard_map/ppermute | solution.py:177
  43.1 2.3 %copy.22 = bf16[3584,68]{0,1:T(8,128)(2,1)} copy(bf16[3584,68]{1,0:T(8,128)(2,1)} %pad_maximum_fusion) | data formatting | bytes 974848
  45.4 2.5 %copy.21 = bf16[3584,64]{0,1:T(8,128)(2,1)} copy(bf16[3584,64]{1,0:T(8,128)(2,1)} %get-tuple-element.5) | data formatting | bytes 917504
  49.3 1.3 constant_dynamic-update-slice_fusion.1
  50.5 1.3 constant_dynamic-update-slice_fusion
  51.8 1.6 %maximum_dynamic-update-slice_fusion = bf16[3584,448]{0,1:T(8,128)(2,1)S(1)} fusion(bf16[3584,448]{0,1:T(8,128)(2,1)S(1)} %constant_dynamic-update-slice_fusion, s32[]{:T(128)S(6)} %select_n.149, bf16[448,448]{0,1:T(8,128)(2,1)} %collective-permute-done.3, bf16[448,448]{0,1:T(8,128)(2,1)} %collective-permute-done.2), kind=kLoop, calls=%fused_computation.27 | loop fusion | flops 1605632 | bytes 1605636 | tf_op jit(solution)/shard_map/dynamic_update_slice | solution.py:190
  53.4 1.3 slice.116
  54.7 1.4 slice_select_fusion
  56.1 24.8 %all-gather.2.cloned.1.call-done = bf16[32,64,3584]{2,1,0:T(8,128)(2,1)} async-done(((bf16[1,64,3584]{2,1,0:T(8,128)(2,1)}), bf16[32,64,3584]{2,1,0:T(8,128)(2,1)}) %all-gather.2.cloned.1.call-update) | async-done | bytes 14680080 | tf_op jit(solution)/shard_map/all_gather | solution.py:221
  80.9 21.4 %fusion.22 = bf16[2048,768]{0,1:T(8,128)(2,1)S(1)} fusion(bf16[2048,3584]{1,0:T(8,128)(2,1)} %bitcast.25, bf16[3584,68]{0,1:T(8,128)(2,1)} %copy.22, bf16[3584,64]{0,1:T(8,128)(2,1)} %copy.21, bf16[3584,224]{0,1:T(8,128)(2,1)} %slice.116, bf16[3584,256]{0,1:T(8,128)(2,1)} %slice_select_fusion), kind=kOutput, calls=%fused_computation.22 | convolution fusion | flops 11325407232 | bytes 22212608 | tf_op jit(solution)/shard_map/dot_general | solution.py:273
  102.3 2.8 %copy.20 = bf16[2048,768]{1,0:T(8,128)(2,1)} copy(bf16[2048,768]{0,1:T(8,128)(2,1)S(1)} %fusion.22) | data formatting | bytes 6291456 | tf_op jit(solution)/shard_map/convert_element_type | solution.py:275
  105.1 15.7 %mixer_scan.1 = bf16[32,64,224]{2,1,0:T(8,128)(2,1)} custom-call(bf16[32,64,768]{2,1,0:T(8,128)(2,1)} %bitcast.20, f32[4,512]{1,0:T(4,128)} %select_maximum_fusion.refs_1_, f32[1,512]{1,0:T(1,128)} %fusion.28.refs_2_, f32[2,128]{1,0:T(2,128)} %select_maximum_fusion.2.refs_3_, f32[1,256]{1,0:T(1,128)} %broadcast_in_dim_reshape.3.refs_4_), custom_call_target="tpu_custom_call" | custom-call | tf_op jit(solution)/shard_map/mixer_scan/pallas_call | solution.py:121
  120.8 5.4 %all-to-all-start = ((bf16[32,64,224]{2,1,0:T(8,128)(2,1)}), bf16[32,64,224]{2,1,0:T(8,128)(2,1)S(1)}, u32[]{:S(2)}, u32[]{:S(2)}) async-start(bf16[32,64,224]{2,1,0:T(8,128)(2,1)} %mixer_scan.1), calls=%async_computation | async-start | bytes 2097152 | tf_op jit(solution)/shard_map/all_to_all | solution.py:278
  127.7 15.4 %all-to-all-done.gated = bf16[32,64,224]{2,1,0:T(8,128)(2,1)S(1)} async-done(((bf16[32,64,224]{2,1,0:T(8,128)(2,1)}), bf16[32,64,224]{2,1,0:T(8,128)(2,1)S(1)}, u32[]{:S(2)}, u32[]{:S(2)}) %all-to-all-start) | async-done | bytes 917536 | tf_op jit(solution)/shard_map/all_to_all | solution.py:278
  144.1 2.8 %gated_norm.1 = bf16[64,7168]{1,0:T(8,128)(2,1)} custom-call(s32[1]{0:T(128)S(6)} %sub.17.limit, bf16[32,64,224]{2,1,0:T(8,128)(2,1)} %copy-done, f32[32,224]{1,0:T(8,128)} %maximum_select_fusion.2.gain), custom_call_target="tpu_custom_call" | custom-call | tf_op jit(solution)/shard_map/gated_norm/pallas_call | solution.py:162
  (59 shorter events, 20.5 us)
Async XLA Ops:
  6.5 74.4 %all-gather.2.cloned.1.call-start = ((), (), s32[]{:S(2)}) async-start(), calls=%async_computation.1 | async-start | bytes 15138816 | tf_op jit(solution)/shard_map/all_gather | solution.py:221
  11.1 5.9 %copy-start.4 = (f32[112]{0:T(128)S(1)}, f32[112]{0:T(128)}, u32[]{:S(2)}) copy-start(f32[112]{0:T(128)} %param.17) | copy-start | bytes 1348
  11.2 6.6 %copy-start.5 = (f32[112]{0:T(128)S(1)}, f32[112]{0:T(128)}, u32[]{:S(2)}) copy-start(f32[112]{0:T(128)} %param.18) | copy-start | bytes 1348
  11.2 7.4 %copy-start.6 = (f32[112]{0:T(128)S(1)}, f32[112]{0:T(128)}, u32[]{:S(2)}) copy-start(f32[112]{0:T(128)} %param.21) | copy-start | bytes 1348
  12.4 23.5 %collective-permute-start = (bf16[896,448]{0,1:T(8,128)(2,1)}, bf16[896,448]{0,1:T(8,128)(2,1)}, u32[]{:S(2)}, u32[]{:S(2)}) collective-permute-start(bf16[896,448]{0,1:T(8,128)(2,1)} %get-tuple-element.7), channel_id=1, source_target_pairs={{0,32},{32,64},{64,96},{96,0},{1,33},{33,65},{65,97},{97,1},{2,34}... | collective-permute-start | bytes 2408456 | tf_op jit(solution)/shard_map/ppermute | solution.py:177
  14.9 22.9 %collective-permute-start.1 = (bf16[896,448]{0,1:T(8,128)(2,1)}, bf16[896,448]{0,1:T(8,128)(2,1)}, u32[]{:S(2)}, u32[]{:S(2)}) collective-permute-start(bf16[896,448]{0,1:T(8,128)(2,1)} %get-tuple-element.7), channel_id=1, source_target_pairs={{0,96},{32,0},{64,32},{96,64},{1,97},{33,1},{65,33},{97,65},{2,98}... | collective-permute-start | bytes 2408456 | tf_op jit(solution)/shard_map/ppermute | solution.py:177
  24.2 10.3 %copy-start.1 = (bf16[3584,4]{1,0:T(8,128)(2,1)S(1)}, bf16[3584,4]{1,0:T(8,128)(2,1)}, u32[]{:S(2)}) copy-start(bf16[3584,4]{1,0:T(8,128)(2,1)} %copy.17) | copy-start | bytes 86020
  37.8 14.0 %collective-permute-start.2 = (bf16[448,448]{0,1:T(8,128)(2,1)}, bf16[448,448]{0,1:T(8,128)(2,1)}, u32[]{:S(2)}, u32[]{:S(2)}) collective-permute-start(bf16[448,448]{0,1:T(8,128)(2,1)} %slice.113), channel_id=1, source_target_pairs={{0,32},{32,64},{64,96},{96,0},{1,33},{33,65},{65,97},{97,1},{2,34}... | collective-permute-start | bytes 1204232 | tf_op jit(solution)/shard_map/ppermute | solution.py:177
  39.8 12.0 %collective-permute-start.3 = (bf16[448,448]{0,1:T(8,128)(2,1)}, bf16[448,448]{0,1:T(8,128)(2,1)}, u32[]{:S(2)}, u32[]{:S(2)}) collective-permute-start(bf16[448,448]{0,1:T(8,128)(2,1)} %slice.114), channel_id=1, source_target_pairs={{0,96},{32,0},{64,32},{96,64},{1,97},{33,1},{65,33},{97,65},{2,98}... | collective-permute-start | bytes 1204232 | tf_op jit(solution)/shard_map/ppermute | solution.py:177
  50.5 4.1 %copy-start.3 = (pred[256]{0:T(512)(128)(4,1)S(1)}, pred[256]{0:T(512)(128)(4,1)}, u32[]{:S(2)}) copy-start(pred[256]{0:T(512)(128)(4,1)} %constant.91.clone.1) | copy-start | bytes 772
  105.1 21.1 %copy-start.2 = (f32[7168]{0:T(1024)S(1)}, f32[7168]{0:T(1024)}, u32[]{:S(2)}) copy-start(f32[7168]{0:T(1024)} %param.22) | copy-start | bytes 86020
  120.8 22.3 %all-to-all-start = ((bf16[32,64,224]{2,1,0:T(8,128)(2,1)}), bf16[32,64,224]{2,1,0:T(8,128)(2,1)S(1)}, u32[]{:S(2)}, u32[]{:S(2)}) async-start(bf16[32,64,224]{2,1,0:T(8,128)(2,1)} %mixer_scan.1), calls=%async_computation | async-start | bytes 2097152 | tf_op jit(solution)/shard_map/all_to_all | solution.py:278
  143.1 1.0 copy-start
Sparse Core Ops, SparseCore 0:
  9.6 71.2 all-gather.1

commit v3 on v2

--- a/solution.py
+++ b/solution.py
@@ -12,7 +12,7 @@
 HEAD = 64
 TILE = 128
 SLOT = 256
-PIECES = 1
+SIDE = 4
 
 
 def split(value):
@@ -25,11 +25,11 @@
 
 
 def scan_kernel(*refs):
-    projected = refs[:PIECES]
-    taps, conv_bias, head_rows, skip, out, xbc, state = refs[PIECES:]
+    parity, first_own, first_other, second_own, second_other = refs[:5]
+    taps, conv_bias, head_rows, skip, out, xbc, state = refs[5:]
     step = pl.program_id(0)
-    rows = projected[0].shape[1]
-    own = rows * PIECES
+    rows = first_own.shape[2]
+    own = rows * 2
     past = xbc.shape[0] - TILE
 
     @pl.when(step == 0)
@@ -42,14 +42,19 @@
         xbc[0:past] = xbc[TILE : TILE + past]
 
     gates = []
-    for owner in range(TILE // own):
-        for piece in range(PIECES):
-            block = projected[piece][owner]
-            start = past + owner * own + piece * rows
-            xbc[start : start + rows, :SLOT] = block[:, :SLOT].astype(jnp.float32)
-            xbc[start : start + rows, SLOT:] = block[:, 2 * SLOT :].astype(jnp.float32)
+    halves = ((first_own, first_other), (second_own, second_other))
+    for core in range(2):
+        for half, (mine, other) in enumerate(halves):
+            block = jnp.where(
+                parity[0] == core,
+                mine[0, 0].astype(jnp.float32),
+                other[0, 0].astype(jnp.float32),
+            )
+            start = past + core * own + half * rows
+            xbc[start : start + rows, :SLOT] = block[:, :SLOT]
+            xbc[start : start + rows, SLOT:] = block[:, 2 * SLOT :]
             gates.append(block[:, SLOT : 2 * SLOT])
-    gate = jnp.concatenate(gates, axis=0).astype(jnp.float32)
+    gate = jnp.concatenate(gates, axis=0)
 
     total = conv_bias[...]
     count = taps.shape[0]
@@ -112,16 +117,19 @@
         state[:, span] = jnp.exp(last) * before[:, span] + block
 
 
-def scan(projected, taps, conv_bias, head_rows, skip, width):
-    owners, rows, columns = projected[0].shape
-    own = rows * PIECES
-    per_step = TILE // own
+def scan(parity, projected, taps, conv_bias, head_rows, skip, width):
+    _, _, rows, columns = projected[0].shape
+    own = rows * 2
+    per_step = 2
+    owners = per_step * SIDE * SIDE
+    by_y = pl.BlockSpec((1, 1, rows, columns), lambda i: (i % SIDE, i // SIDE, 0, 0))
+    by_x = pl.BlockSpec((1, 1, rows, columns), lambda i: (i // SIDE, i % SIDE, 0, 0))
     whole = lambda array: pl.BlockSpec(array.shape, lambda i: (0,) * array.ndim)
     constants = (taps, conv_bias, head_rows, skip)
     return pl.pallas_call(
         scan_kernel,
         grid=(owners // per_step,),
-        in_specs=[pl.BlockSpec((per_step, rows, columns), lambda i: (i, 0, 0))] * PIECES
+        in_specs=[pl.BlockSpec(memory_space=pltpu.SMEM), by_y, by_y, by_x, by_x]
         + [whole(array) for array in constants],
         out_specs=pl.BlockSpec((per_step, own, width), lambda i: (i, 0, 0)),
         out_shape=jax.ShapeDtypeStruct((owners, own, width), jnp.bfloat16),
@@ -130,7 +138,7 @@
             pltpu.VMEM((TILE, SLOT), jnp.float32),
         ],
         name="mixer_scan",
-    )(*projected, *constants)
+    )(parity, *projected, *constants)
 
 
 def norm_kernel(turned, limit, gated, gain, out):
@@ -188,6 +196,33 @@
     whole = jnp.zeros((4 * depth,) + block.shape[1:], block.dtype)
     for distance, part in ((0, block), (3, behind), (1, ahead), (2, far)):
         whole = lax.dynamic_update_slice(whole, part, ((me + distance) % 4 * depth, 0))
+    return whole
+
+
+def move(block, dx, dy, across=0):
+    pairs = []
+    for x in range(SIDE):
+        for y in range(SIDE):
+            for core in range(2):
+                target = ((x + dx) % SIDE * SIDE + (y + dy) % SIDE) * 2 + (core + across) % 2
+                pairs.append(((x * SIDE + y) * 2 + core, target))
+    return lax.ppermute(block, "seq", pairs)
+
+
+def line(block, dx, dy):
+    half = block.shape[0] // 2
+    behind, ahead = move(block, dx, dy), move(block, -dx, -dy)
+    far = jnp.concatenate(
+        [move(behind[:half], dx, dy), move(ahead[half:], -dx, -dy)], axis=0
+    )
+    return block, ahead, far, behind
+
+
+def place(parts, position):
+    rows = parts[0].shape[0]
+    whole = jnp.zeros((SIDE * rows,) + parts[0].shape[1:], parts[0].dtype)
+    for distance, part in enumerate(parts):
+        whole = lax.dynamic_update_slice(whole, part, ((position + distance) % SIDE * rows, 0))
     return whole
 
 
@@ -216,10 +251,12 @@
     inner = norm_gain.shape[0]
     group = me // (owners // GROUPS)
 
-    rows = num_rows // PIECES
-    token_pieces = [
-        lax.all_gather(own_rows[j * rows : (j + 1) * rows], "seq") for j in range(PIECES)
-    ]
+    at_x, at_y = me // (2 * SIDE), me // 2 % SIDE
+    rows = num_rows // 2
+    column = place(line(own_rows[:rows], 1, 0), at_x)
+    row = place(line(own_rows[rows:], 0, 1), at_y)
+    first_parts = line(column, 0, 1)
+    second_parts = line(row, 1, 0)
 
     def turn(columns):
         return jnp.where(odd, jnp.roll(columns, -turned, axis=-1), columns)
@@ -268,13 +305,19 @@
         (jnp.arange(owners) % 2 == 1)[:, None], jnp.roll(gains, -turned, axis=1), gains
     )
 
+    def project(parts, position):
+        blocks = [
+            jnp.dot(part, weights, preferred_element_type=jnp.float32).astype(jnp.bfloat16)
+            for part in parts
+        ]
+        return place(blocks, position).reshape(SIDE, SIDE, rows, -1)
+
     projected = []
-    for piece in token_pieces:
-        block = jnp.dot(
-            piece.reshape(owners * rows, depth), weights, preferred_element_type=jnp.float32
-        ).astype(jnp.bfloat16)
-        projected.append(block.reshape(owners, rows, -1))
-    gated = scan(projected, taps, bias, head_rows, skip, width)
+    for parts, position in ((first_parts, at_y), (second_parts, at_x)):
+        projected.append(project(parts, position))
+        projected.append(project([move(part, 0, 0, 1) for part in parts], position))
+    parity = (me % 2)[None]
+    gated = scan(parity, projected, taps, bias, head_rows, skip, width)
     mine = lax.all_to_all(gated, "seq", split_axis=0, concat_axis=0, tiled=True)
     limit = lengths - me * num_rows
     return norm(limit, mine, gains, turned)[None]

time: 155 us -> 182 us (1.17)
  starting transfers between devices: 12.7 us -> 41.8 us
  between operations: 14.2 us -> 1.25 us
  matrix products: 21.4 us -> 31.9 us
  waiting for transfers between devices: 41 us -> 30.5 us
  local copies, waits for them, and re-layouts: 33.5 us -> 42.7 us
    ppermute x0 -> x24, starting transfers between devices: none -> 31.2 us  [move(): return lax.ppermute(block, 'seq', pairs)]
    all_gather x1 -> x0, waiting for transfers between devices: 24.8 us -> none  [local(): lax.all_gather(own_rows[j * rows:(j + 1) * rows], 'seq')]
    ppermute x0 -> x24, waiting for transfers between devices: none -> 11.2 us  [move(): return lax.ppermute(block, 'seq', pairs)]
    dot_general x1 -> x16, matrix products: 21.4 us -> 31.9 us  [project(): jnp.dot(part, weights, preferred_element_type=jnp.float32)]
    dynamic_update_slice x0 -> x6, local copies, waits for them, and re-layouts: none -> 7.98 us  [place(): lax.dynamic_update_slice(whole, part, ((position + distance) % SIDE * row...]
    ppermute x4, waiting for transfers between devices: 0.01 us -> 3.87 us  [around(): lax.ppermute(block, axis, [(i, (i + distance) % size) for i in range(size)])]
    slice x0 -> x9, local copies, waits for them, and re-layouts: none -> 3.85 us  [the longest x1 1.9 us: local(): row = place(line(own_rows[rows:], 0, 1), at_y)]
    convert_element_type x1 -> x0, local copies, waits for them, and re-layouts: 2.83 us -> none  [local(): block = jnp.dot(piece.reshape(owners * rows, depth), weights, preferred_e...]
  transfers between devices with their start and end apart: 6 -> 29, of which waited for: 2 -> 4; matrix products, arithmetic and copies ran while one was open for 27% -> 46% of each run, Pallas kernels for 0% -> 0%
where the time goes in v3:
time: 182 us; the launch traced here: 180 us
  local copies, waits for them, and re-layouts  42.7 us (23%)
  starting transfers between devices  41.8 us (23%)
  matrix products  31.9 us (18%)
  waiting for transfers between devices  30.5 us (17%)
  Pallas kernels  18.7 us (10%)
  other arithmetic  13.3 us (7%)
    dot_general x16, matrix products, project(): jnp.dot(part, weights, preferred_element_type=jnp.float32)  31.9 us
    ppermute x24, starting transfers between devices, move(): return lax.ppermute(block, 'seq', pairs)  31.2 us
    pallas_call x1, Pallas kernels, scan(): pl.pallas_call(scan_kernel, grid=(owners // per_step,), in_specs=[pl.Bloc...  15.9 us
    all_to_all x1, waiting for transfers between devices, local(): mine = lax.all_to_all(gated, 'seq', split_axis=0, concat_axis=0, tiled=True)  15.5 us
    ppermute x24, waiting for transfers between devices, move(): return lax.ppermute(block, 'seq', pairs)  11.2 us
    dynamic_update_slice x6, local copies, waits for them, and re-layouts, place(): lax.dynamic_update_slice(whole, part, ((position + distance) % SIDE * row...  7.98 us
    ppermute x4, starting transfers between devices, around(): lax.ppermute(block, axis, [(i, (i + distance) % size) for i in range(size)])  6.56 us
    unnamed x28, local copies, waits for them, and re-layouts  6.56 us
  transfers between devices with their start and end apart: 29, of which 4 were waited for; matrix products, arithmetic and copies ran while one was open for 46% of the time, Pallas kernels for 0%

profile of v3, /device:TPU:1, one launch (start us, length us, event | category | flops | bytes accessed | tf_op | source)
XLA Modules:
  0.0 180.2 jit_solution(5536952924402433675)
XLA Ops:
  0.0 1.9 %slice_bitcast_fusion = (bf16[32,3584]{1,0:T(8,128)(2,1)}, bf16[32,3584]{1,0:T(8,128)(2,1)}) fusion(bf16[1,64,3584]{2,1,0:T(8,128)(2,1)} %param.12), kind=kLoop, calls=%fused_computation.53 | loop fusion | bytes 917504 | tf_op jit(solution)/shard_map/slice | solution.py:257
  1.9 3.6 %collective-permute-start.16 = (bf16[32,3584]{1,0:T(8,128)(2,1)}, bf16[32,3584]{1,0:T(8,128)(2,1)}, u32[]{:S(2)}, u32[]{:S(2)}) collective-permute-start(bf16[32,3584]{1,0:T(8,128)(2,1)} %get-tuple-element.9), channel_id=1, source_target_pairs={{0,6},{1,7},{2,0},{3,1},{4,2},{5,3},{6,4},{7,5},{8,14},{9,15},{10,... | collective-permute-start | bytes 688136 | tf_op jit(solution)/shard_map/ppermute | solution.py:209
  12.2 2.1 %collective-permute-start.5 = (bf16[896,448]{0,1:T(8,128)(2,1)}, bf16[896,448]{0,1:T(8,128)(2,1)}, u32[]{:S(2)}, u32[]{:S(2)}) collective-permute-start(bf16[896,448]{0,1:T(8,128)(2,1)} %get-tuple-element.7), channel_id=1, source_target_pairs={{0,96},{32,0},{64,32},{96,64},{1,97},{33,1},{65,33},{97,65},{2,98}... | collective-permute-start | bytes 2408456 | tf_op jit(solution)/shard_map/ppermute | solution.py:185
  28.6 2.9 %constant_dynamic-slice_fusion.8 = (bf16[3584,64]{1,0:T(8,128)(2,1)}, bf16[3584,64]{1,0:T(8,128)(2,1)S(1)}) fusion(bf16[3584,256]{1,0:T(8,128)(2,1)} %param.15, s32[]{:T(128)S(6)} %select_n.290, s32[]{:T(128)S(6)} %select_n.291), kind=kLoop, calls=%fused_computation.74 | loop fusion | bytes 1835016 | tf_op jit(solution)/shard_map/dynamic_slice | solution.py:274
  31.6 2.6 %pad_maximum_fusion = bf16[3584,68]{1,0:T(8,128)(2,1)} fusion(bf16[3584,4]{1,0:T(8,128)(2,1)} %copy.13, bf16[3584,64]{1,0:T(8,128)(2,1)S(1)} %get-tuple-element.6), kind=kLoop, calls=%fused_computation.46 | loop fusion | flops 974848 | bytes 974848 | tf_op jit(solution)/shard_map/concatenate | solution.py:287
  40.8 2.3 %copy.17 = bf16[3584,68]{0,1:T(8,128)(2,1)} copy(bf16[3584,68]{1,0:T(8,128)(2,1)} %pad_maximum_fusion) | data formatting | bytes 974848
  43.1 2.2 %copy.16 = bf16[3584,64]{0,1:T(8,128)(2,1)} copy(bf16[3584,64]{1,0:T(8,128)(2,1)} %get-tuple-element.5) | data formatting | bytes 917504
  49.9 2.7 %collective-permute-start.19 = (bf16[16,3584]{1,0:T(8,128)(2,1)S(1)}, bf16[16,3584]{1,0:T(8,128)(2,1)S(1)}, u32[]{:S(2)}, u32[]{:S(2)}) collective-permute-start(bf16[16,3584]{1,0:T(8,128)(2,1)S(1)} %slice.170), channel_id=1, source_target_pairs={{0,6},{1,7},{2,0},{3,1},{4,2},{5,3},{6,4},{7,5},{8,14},{9,15},{10,... | collective-permute-start | bytes 344072 | tf_op jit(solution)/shard_map/ppermute | solution.py:209
  56.0 2.7 %collective-permute-start.3 = (bf16[16,3584]{1,0:T(8,128)(2,1)S(1)}, bf16[16,3584]{1,0:T(8,128)(2,1)S(1)}, u32[]{:S(2)}, u32[]{:S(2)}) collective-permute-start(bf16[16,3584]{1,0:T(8,128)(2,1)S(1)} %slice.162), channel_id=1, source_target_pairs={{0,24},{1,25},{2,26},{3,27},{4,28},{5,29},{6,30},{7,31},{8,0},{9,1... | collective-permute-start | bytes 344072 | tf_op jit(solution)/shard_map/ppermute | solution.py:209
  60.1 4.0 %collective-permute-start.24 = (bf16[128,3584]{1,0:T(8,128)(2,1)}, bf16[128,3584]{1,0:T(8,128)(2,1)S(1)}, u32[]{:S(2)}, u32[]{:S(2)}) collective-permute-start(bf16[128,3584]{1,0:T(8,128)(2,1)} %constant_dynamic-update-slice_fusion.4), channel_id=1, source_target_pairs={{0,1},{1,0},{2,3},{3,2},{4,5},{5,4},{6,7},{7,6},{8,9},{9,8},{10,11... | collective-permute-start | bytes 2752520 | tf_op jit(solution)/shard_map/ppermute | solution.py:209
  68.7 2.7 %collective-permute-start.7 = (bf16[448,448]{0,1:T(8,128)(2,1)S(1)}, bf16[448,448]{0,1:T(8,128)(2,1)S(1)}, u32[]{:S(2)}, u32[]{:S(2)}) collective-permute-start(bf16[448,448]{0,1:T(8,128)(2,1)S(1)} %slice.164), channel_id=1, source_target_pairs={{0,96},{32,0},{64,32},{96,64},{1,97},{33,1},{65,33},{97,65},{2,98}... | collective-permute-start | bytes 1204232 | tf_op jit(solution)/shard_map/ppermute | solution.py:185
  75.7 3.9 %collective-permute-done.6 = bf16[448,448]{0,1:T(8,128)(2,1)S(1)} collective-permute-done((bf16[448,448]{0,1:T(8,128)(2,1)S(1)}, bf16[448,448]{0,1:T(8,128)(2,1)S(1)}, u32[]{:S(2)}, u32[]{:S(2)}) %collective-permute-start.6) | collective-permute-done | bytes 401440 | tf_op jit(solution)/shard_map/ppermute | solution.py:185
  82.3 3.0 %fusion.15 = bf16[512,768]{1,0:T(8,128)(2,1)S(1)} fusion(bf16[512,768]{1,0:T(8,128)(2,1)S(1)} %broadcast.75.clone.2, s32[]{:T(128)S(6)} %select_n.309, bf16[128,3584]{1,0:T(8,128)(2,1)} %constant_dynamic-update-slice_fusion.4, bf16[3584,768]{0,1:T(8,128)(2,1)S(1)} %fusion.6), kind=kOutput, calls=%fused_computation.29 | convolution fusion | flops 704741376 | bytes 6619140 | tf_op jit(solution)/shard_map/dot_general | solution.py:310
  86.2 2.2 %collective-permute-start.12 = (bf16[128,3584]{1,0:T(8,128)(2,1)}, bf16[128,3584]{1,0:T(8,128)(2,1)S(1)}, u32[]{:S(2)}, u32[]{:S(2)}) collective-permute-start(bf16[128,3584]{1,0:T(8,128)(2,1)} %constant_dynamic-update-slice_fusion.10), channel_id=1, source_target_pairs={{0,1},{1,0},{2,3},{3,2},{4,5},{5,4},{6,7},{7,6},{8,9},{9,8},{10,11... | collective-permute-start | bytes 2752520 | tf_op jit(solution)/shard_map/ppermute | solution.py:209
  88.5 3.0 %fusion.23 = bf16[512,768]{1,0:T(8,128)(2,1)S(1)} fusion(bf16[512,768]{1,0:T(8,128)(2,1)S(1)} %broadcast.75.clone, s32[]{:T(128)S(6)} %select_n.298, bf16[128,3584]{1,0:T(8,128)(2,1)} %constant_dynamic-update-slice_fusion.10, bf16[3584,768]{0,1:T(8,128)(2,1)S(1)} %fusion.6), kind=kOutput, calls=%fused_computation.45 | convolution fusion | flops 704741376 | bytes 6619140 | tf_op jit(solution)/shard_map/dot_general | solution.py:310
  91.8 10.3 %collective-permute-done.9 = bf16[128,3584]{1,0:T(8,128)(2,1)S(1)} collective-permute-done((bf16[128,3584]{1,0:T(8,128)(2,1)}, bf16[128,3584]{1,0:T(8,128)(2,1)S(1)}, u32[]{:S(2)}, u32[]{:S(2)}) %collective-permute-start.9) | collective-permute-done | bytes 917536 | tf_op jit(solution)/shard_map/ppermute | solution.py:209
  103.3 2.7 %collective-permute-start.11 = (bf16[64,3584]{1,0:T(8,128)(2,1)S(1)}, bf16[64,3584]{1,0:T(8,128)(2,1)S(1)}, u32[]{:S(2)}, u32[]{:S(2)}) collective-permute-start(bf16[64,3584]{1,0:T(8,128)(2,1)S(1)} %slice.168), channel_id=1, source_target_pairs={{0,6},{1,7},{2,0},{3,1},{4,2},{5,3},{6,4},{7,5},{8,14},{9,15},{10,... | collective-permute-start | bytes 1376264 | tf_op jit(solution)/shard_map/ppermute | solution.py:209
  108.0 1.8 %fusion.14 = bf16[512,768]{1,0:T(8,128)(2,1)S(1)} fusion(bf16[512,768]{1,0:T(8,128)(2,1)S(1)} %fusion.15, s32[]{:T(128)S(6)} %select_n.310, bf16[128,3584]{1,0:T(8,128)(2,1)S(1)} %collective-permute-done.20, bf16[3584,768]{0,1:T(8,128)(2,1)S(1)} %fusion.6), kind=kOutput, calls=%fused_computation.27 | convolution fusion | flops 704741376 | bytes 6619140 | tf_op jit(solution)/shard_map/dot_general | solution.py:310
  109.8 4.4 %collective-permute-start.25 = (bf16[128,3584]{1,0:T(8,128)(2,1)S(1)}, bf16[128,3584]{1,0:T(8,128)(2,1)S(1)}, u32[]{:S(2)}, u32[]{:S(2)}) collective-permute-start(bf16[128,3584]{1,0:T(8,128)(2,1)S(1)} %collective-permute-done.20), channel_id=1, source_target_pairs={{0,1},{1,0},{2,3},{3,2},{4,5},{5,4},{6,7},{7,6},{8,9},{9,8},{10,11... | collective-permute-start | bytes 2752520 | tf_op jit(solution)/shard_map/ppermute | solution.py:209
  136.6 1.8 %fusion.16 = bf16[512,768]{1,0:T(8,128)(2,1)S(1)} fusion(bf16[512,768]{1,0:T(8,128)(2,1)S(1)} %fusion.17, s32[]{:T(128)S(6)} %select_n.304, bf16[128,3584]{1,0:T(8,128)(2,1)S(1)} %collective-permute-done.15, bf16[3584,768]{0,1:T(8,128)(2,1)S(1)} %fusion.6), kind=kOutput, calls=%fused_computation.31 | convolution fusion | flops 704741376 | bytes 6619140 | tf_op jit(solution)/shard_map/dot_general | solution.py:310
  139.4 15.9 %mixer_scan.1 = bf16[32,64,224]{2,1,0:T(8,128)(2,1)} custom-call(s32[1]{0:T(128)} %bitcast.1.refs_0_, bf16[4,4,32,768]{3,2,1,0:T(8,128)(2,1)} %bitcast.63, bf16[4,4,32,768]{3,2,1,0:T(8,128)(2,1)} %bitcast.60, bf16[4,4,32,768]{3,2,1,0:T(8,128)(2,1)} %bitcast.62, bf16[4,4,32,768]{3,2,1,0:T(8,128)(2,1)} %bitcast.61, f32[4,512]{1,0:T(4,128)} %select_maximum_fusion.refs_5_, ...), custom_call_target="tpu_custom_call" | custom-call | tf_op jit(solution)/shard_map/mixer_scan/pallas_call | solution.py:129
  155.3 4.1 %all-to-all-start = ((bf16[32,64,224]{2,1,0:T(8,128)(2,1)}), bf16[32,64,224]{2,1,0:T(8,128)(2,1)S(1)}, u32[]{:S(2)}, u32[]{:S(2)}) async-start(bf16[32,64,224]{2,1,0:T(8,128)(2,1)} %mixer_scan.1), calls=%async_computation | async-start | bytes 2097152 | tf_op jit(solution)/shard_map/all_to_all | solution.py:321
  160.9 15.5 %all-to-all-done.gated = bf16[32,64,224]{2,1,0:T(8,128)(2,1)S(1)} async-done(((bf16[32,64,224]{2,1,0:T(8,128)(2,1)}), bf16[32,64,224]{2,1,0:T(8,128)(2,1)S(1)}, u32[]{:S(2)}, u32[]{:S(2)}) %all-to-all-start) | async-done | bytes 917536 | tf_op jit(solution)/shard_map/all_to_all | solution.py:321
  177.4 2.8 %gated_norm.1 = bf16[64,7168]{1,0:T(8,128)(2,1)} custom-call(s32[1]{0:T(128)S(6)} %sub.21.limit, bf16[32,64,224]{2,1,0:T(8,128)(2,1)} %copy-done, f32[32,224]{1,0:T(8,128)} %maximum_select_fusion.2.gain), custom_call_target="tpu_custom_call" | custom-call | tf_op jit(solution)/shard_map/gated_norm/pallas_call | solution.py:170
  (156 shorter events, 77.6 us)
Async XLA Ops:
  1.9 47.0 %collective-permute-start.16 = (bf16[32,3584]{1,0:T(8,128)(2,1)}, bf16[32,3584]{1,0:T(8,128)(2,1)}, u32[]{:S(2)}, u32[]{:S(2)}) collective-permute-start(bf16[32,3584]{1,0:T(8,128)(2,1)} %get-tuple-element.9), channel_id=1, source_target_pairs={{0,6},{1,7},{2,0},{3,1},{4,2},{5,3},{6,4},{7,5},{8,14},{9,15},{10,... | collective-permute-start | bytes 688136 | tf_op jit(solution)/shard_map/ppermute | solution.py:209
  5.5 42.0 %collective-permute-start.17 = (bf16[32,3584]{1,0:T(8,128)(2,1)}, bf16[32,3584]{1,0:T(8,128)(2,1)S(1)}, u32[]{:S(2)}, u32[]{:S(2)}) collective-permute-start(bf16[32,3584]{1,0:T(8,128)(2,1)} %get-tuple-element.9), channel_id=1, source_target_pairs={{0,2},{1,3},{2,4},{3,5},{4,6},{5,7},{6,0},{7,1},{8,10},{9,11},{10,... | collective-permute-start | bytes 688136 | tf_op jit(solution)/shard_map/ppermute | solution.py:209
  10.6 55.7 %collective-permute-start.4 = (bf16[896,448]{0,1:T(8,128)(2,1)}, bf16[896,448]{0,1:T(8,128)(2,1)}, u32[]{:S(2)}, u32[]{:S(2)}) collective-permute-start(bf16[896,448]{0,1:T(8,128)(2,1)} %get-tuple-element.7), channel_id=1, source_target_pairs={{0,32},{32,64},{64,96},{96,0},{1,33},{33,65},{65,97},{97,1},{2,34}... | collective-permute-start | bytes 2408456 | tf_op jit(solution)/shard_map/ppermute | solution.py:185
  12.2 55.2 %collective-permute-start.5 = (bf16[896,448]{0,1:T(8,128)(2,1)}, bf16[896,448]{0,1:T(8,128)(2,1)}, u32[]{:S(2)}, u32[]{:S(2)}) collective-permute-start(bf16[896,448]{0,1:T(8,128)(2,1)} %get-tuple-element.7), channel_id=1, source_target_pairs={{0,96},{32,0},{64,32},{96,64},{1,97},{33,1},{65,33},{97,65},{2,98}... | collective-permute-start | bytes 2408456 | tf_op jit(solution)/shard_map/ppermute | solution.py:185
  14.4 35.6 %collective-permute-start.1 = (bf16[32,3584]{1,0:T(8,128)(2,1)}, bf16[32,3584]{1,0:T(8,128)(2,1)}, u32[]{:S(2)}, u32[]{:S(2)}) collective-permute-start(bf16[32,3584]{1,0:T(8,128)(2,1)} %get-tuple-element.10), channel_id=1, source_target_pairs={{0,8},{1,9},{2,10},{3,11},{4,12},{5,13},{6,14},{7,15},{8,16},{9,17... | collective-permute-start | bytes 688136 | tf_op jit(solution)/shard_map/ppermute | solution.py:209
  55.2 8.9 %collective-permute-start.2 = (bf16[16,3584]{1,0:T(8,128)(2,1)S(1)}, bf16[16,3584]{1,0:T(8,128)(2,1)S(1)}, u32[]{:S(2)}, u32[]{:S(2)}) collective-permute-start(bf16[16,3584]{1,0:T(8,128)(2,1)S(1)} %slice.161), channel_id=1, source_target_pairs={{0,8},{1,9},{2,10},{3,11},{4,12},{5,13},{6,14},{7,15},{8,16},{9,17... | collective-permute-start | bytes 344072 | tf_op jit(solution)/shard_map/ppermute | solution.py:209
  60.1 43.2 %collective-permute-start.24 = (bf16[128,3584]{1,0:T(8,128)(2,1)}, bf16[128,3584]{1,0:T(8,128)(2,1)S(1)}, u32[]{:S(2)}, u32[]{:S(2)}) collective-permute-start(bf16[128,3584]{1,0:T(8,128)(2,1)} %constant_dynamic-update-slice_fusion.4), channel_id=1, source_target_pairs={{0,1},{1,0},{2,3},{3,2},{4,5},{5,4},{6,7},{7,6},{8,9},{9,8},{10,11... | collective-permute-start | bytes 2752520 | tf_op jit(solution)/shard_map/ppermute | solution.py:209
  64.1 27.4 %collective-permute-start.20 = (bf16[128,3584]{1,0:T(8,128)(2,1)}, bf16[128,3584]{1,0:T(8,128)(2,1)S(1)}, u32[]{:S(2)}, u32[]{:S(2)}) collective-permute-start(bf16[128,3584]{1,0:T(8,128)(2,1)} %constant_dynamic-update-slice_fusion.4), channel_id=1, source_target_pairs={{0,24},{1,25},{2,26},{3,27},{4,28},{5,29},{6,30},{7,31},{8,0},{9,1... | collective-permute-start | bytes 2752520 | tf_op jit(solution)/shard_map/ppermute | solution.py:209
  64.2 22.0 %collective-permute-start.21 = (bf16[128,3584]{1,0:T(8,128)(2,1)}, bf16[128,3584]{1,0:T(8,128)(2,1)S(1)}, u32[]{:S(2)}, u32[]{:S(2)}) collective-permute-start(bf16[128,3584]{1,0:T(8,128)(2,1)} %constant_dynamic-update-slice_fusion.4), channel_id=1, source_target_pairs={{0,8},{1,9},{2,10},{3,11},{4,12},{5,13},{6,14},{7,15},{8,16},{9,17... | collective-permute-start | bytes 2752520 | tf_op jit(solution)/shard_map/ppermute | solution.py:209
  67.4 12.2 %collective-permute-start.6 = (bf16[448,448]{0,1:T(8,128)(2,1)S(1)}, bf16[448,448]{0,1:T(8,128)(2,1)S(1)}, u32[]{:S(2)}, u32[]{:S(2)}) collective-permute-start(bf16[448,448]{0,1:T(8,128)(2,1)S(1)} %slice.163), channel_id=1, source_target_pairs={{0,32},{32,64},{64,96},{96,0},{1,33},{33,65},{65,97},{97,1},{2,34}... | collective-permute-start | bytes 1204232 | tf_op jit(solution)/shard_map/ppermute | solution.py:185
  68.7 12.4 %collective-permute-start.7 = (bf16[448,448]{0,1:T(8,128)(2,1)S(1)}, bf16[448,448]{0,1:T(8,128)(2,1)S(1)}, u32[]{:S(2)}, u32[]{:S(2)}) collective-permute-start(bf16[448,448]{0,1:T(8,128)(2,1)S(1)} %slice.164), channel_id=1, source_target_pairs={{0,96},{32,0},{64,32},{96,64},{1,97},{33,1},{65,33},{97,65},{2,98}... | collective-permute-start | bytes 1204232 | tf_op jit(solution)/shard_map/ppermute | solution.py:185
  79.6 23.6 %collective-permute-start.8 = (bf16[128,3584]{1,0:T(8,128)(2,1)}, bf16[128,3584]{1,0:T(8,128)(2,1)S(1)}, u32[]{:S(2)}, u32[]{:S(2)}) collective-permute-start(bf16[128,3584]{1,0:T(8,128)(2,1)} %constant_dynamic-update-slice_fusion.10), channel_id=1, source_target_pairs={{0,6},{1,7},{2,0},{3,1},{4,2},{5,3},{6,4},{7,5},{8,14},{9,15},{10,... | collective-permute-start | bytes 2752520 | tf_op jit(solution)/shard_map/ppermute | solution.py:209
  81.1 21.0 %collective-permute-start.9 = (bf16[128,3584]{1,0:T(8,128)(2,1)}, bf16[128,3584]{1,0:T(8,128)(2,1)S(1)}, u32[]{:S(2)}, u32[]{:S(2)}) collective-permute-start(bf16[128,3584]{1,0:T(8,128)(2,1)} %constant_dynamic-update-slice_fusion.10), channel_id=1, source_target_pairs={{0,2},{1,3},{2,4},{3,5},{4,6},{5,7},{6,0},{7,1},{8,10},{9,11},{10,... | collective-permute-start | bytes 2752520 | tf_op jit(solution)/shard_map/ppermute | solution.py:209
  86.2 23.6 %collective-permute-start.12 = (bf16[128,3584]{1,0:T(8,128)(2,1)}, bf16[128,3584]{1,0:T(8,128)(2,1)S(1)}, u32[]{:S(2)}, u32[]{:S(2)}) collective-permute-start(bf16[128,3584]{1,0:T(8,128)(2,1)} %constant_dynamic-update-slice_fusion.10), channel_id=1, source_target_pairs={{0,1},{1,0},{2,3},{3,2},{4,5},{5,4},{6,7},{7,6},{8,9},{9,8},{10,11... | collective-permute-start | bytes 2752520 | tf_op jit(solution)/shard_map/ppermute | solution.py:209
  91.6 26.4 %collective-permute-start.22 = (bf16[64,3584]{1,0:T(8,128)(2,1)S(1)}, bf16[64,3584]{1,0:T(8,128)(2,1)S(1)}, u32[]{:S(2)}, u32[]{:S(2)}) collective-permute-start(bf16[64,3584]{1,0:T(8,128)(2,1)S(1)} %slice.171), channel_id=1, source_target_pairs={{0,8},{1,9},{2,10},{3,11},{4,12},{5,13},{6,14},{7,15},{8,16},{9,17... | collective-permute-start | bytes 1376264 | tf_op jit(solution)/shard_map/ppermute | solution.py:209
  102.1 16.0 %collective-permute-start.23 = (bf16[64,3584]{1,0:T(8,128)(2,1)S(1)}, bf16[64,3584]{1,0:T(8,128)(2,1)S(1)}, u32[]{:S(2)}, u32[]{:S(2)}) collective-permute-start(bf16[64,3584]{1,0:T(8,128)(2,1)S(1)} %slice.172), channel_id=1, source_target_pairs={{0,24},{1,25},{2,26},{3,27},{4,28},{5,29},{6,30},{7,31},{8,0},{9,1... | collective-permute-start | bytes 1376264 | tf_op jit(solution)/shard_map/ppermute | solution.py:209
  103.2 17.4 %collective-permute-start.10 = (bf16[64,3584]{1,0:T(8,128)(2,1)S(1)}, bf16[64,3584]{1,0:T(8,128)(2,1)S(1)}, u32[]{:S(2)}, u32[]{:S(2)}) collective-permute-start(bf16[64,3584]{1,0:T(8,128)(2,1)S(1)} %slice.167), channel_id=1, source_target_pairs={{0,2},{1,3},{2,4},{3,5},{4,6},{5,7},{6,0},{7,1},{8,10},{9,11},{10,... | collective-permute-start | bytes 1376264 | tf_op jit(solution)/shard_map/ppermute | solution.py:209
  103.3 17.4 %collective-permute-start.11 = (bf16[64,3584]{1,0:T(8,128)(2,1)S(1)}, bf16[64,3584]{1,0:T(8,128)(2,1)S(1)}, u32[]{:S(2)}, u32[]{:S(2)}) collective-permute-start(bf16[64,3584]{1,0:T(8,128)(2,1)S(1)} %slice.168), channel_id=1, source_target_pairs={{0,6},{1,7},{2,0},{3,1},{4,2},{5,3},{6,4},{7,5},{8,14},{9,15},{10,... | collective-permute-start | bytes 1376264 | tf_op jit(solution)/shard_map/ppermute | solution.py:209
  109.8 17.1 %collective-permute-start.25 = (bf16[128,3584]{1,0:T(8,128)(2,1)S(1)}, bf16[128,3584]{1,0:T(8,128)(2,1)S(1)}, u32[]{:S(2)}, u32[]{:S(2)}) collective-permute-start(bf16[128,3584]{1,0:T(8,128)(2,1)S(1)} %collective-permute-done.20), channel_id=1, source_target_pairs={{0,1},{1,0},{2,3},{3,2},{4,5},{5,4},{6,7},{7,6},{8,9},{9,8},{10,11... | collective-permute-start | bytes 2752520 | tf_op jit(solution)/shard_map/ppermute | solution.py:209
  118.0 14.9 %collective-permute-start.27 = (bf16[128,3584]{1,0:T(8,128)(2,1)S(1)}, bf16[128,3584]{1,0:T(8,128)(2,1)S(1)}, u32[]{:S(2)}, u32[]{:S(2)}) collective-permute-start(bf16[128,3584]{1,0:T(8,128)(2,1)S(1)} %collective-permute-done.21), channel_id=1, source_target_pairs={{0,1},{1,0},{2,3},{3,2},{4,5},{5,4},{6,7},{7,6},{8,9},{9,8},{10,11... | collective-permute-start | bytes 2752520 | tf_op jit(solution)/shard_map/ppermute | solution.py:209
  118.1 11.0 %collective-permute-start.13 = (bf16[128,3584]{1,0:T(8,128)(2,1)S(1)}, bf16[128,3584]{1,0:T(8,128)(2,1)S(1)}, u32[]{:S(2)}, u32[]{:S(2)}) collective-permute-start(bf16[128,3584]{1,0:T(8,128)(2,1)S(1)} %collective-permute-done.8), channel_id=1, source_target_pairs={{0,1},{1,0},{2,3},{3,2},{4,5},{5,4},{6,7},{7,6},{8,9},{9,8},{10,11... | collective-permute-start | bytes 2752520 | tf_op jit(solution)/shard_map/ppermute | solution.py:209
  120.6 16.0 %collective-permute-start.15 = (bf16[128,3584]{1,0:T(8,128)(2,1)S(1)}, bf16[128,3584]{1,0:T(8,128)(2,1)S(1)}, u32[]{:S(2)}, u32[]{:S(2)}) collective-permute-start(bf16[128,3584]{1,0:T(8,128)(2,1)S(1)} %collective-permute-done.9), channel_id=1, source_target_pairs={{0,1},{1,0},{2,3},{3,2},{4,5},{5,4},{6,7},{7,6},{8,9},{9,8},{10,11... | collective-permute-start | bytes 2752520 | tf_op jit(solution)/shard_map/ppermute | solution.py:209
  120.7 10.2 %collective-permute-start.26 = (bf16[128,3584]{1,0:T(8,128)(2,1)S(1)}, bf16[128,3584]{1,0:T(8,128)(2,1)S(1)}, u32[]{:S(2)}, u32[]{:S(2)}) collective-permute-start(bf16[128,3584]{1,0:T(8,128)(2,1)S(1)} %constant_dynamic-update-slice_fusion.2), channel_id=1, source_target_pairs={{0,1},{1,0},{2,3},{3,2},{4,5},{5,4},{6,7},{7,6},{8,9},{9,8},{10,11... | collective-permute-start | bytes 2752520 | tf_op jit(solution)/shard_map/ppermute | solution.py:209
  155.3 21.1 %all-to-all-start = ((bf16[32,64,224]{2,1,0:T(8,128)(2,1)}), bf16[32,64,224]{2,1,0:T(8,128)(2,1)S(1)}, u32[]{:S(2)}, u32[]{:S(2)}) async-start(bf16[32,64,224]{2,1,0:T(8,128)(2,1)} %mixer_scan.1), calls=%async_computation | async-start | bytes 2097152 | tf_op jit(solution)/shard_map/all_to_all | solution.py:321
  (17 other events, 164.7 us)

commit v4 on v3

--- a/solution.py
+++ b/solution.py
@@ -25,10 +25,10 @@
 
 
 def scan_kernel(*refs):
-    parity, first_own, first_other, second_own, second_other = refs[:5]
-    taps, conv_bias, head_rows, skip, out, xbc, state = refs[5:]
+    parity, first, second_own, second_other = refs[:4]
+    taps, conv_bias, head_rows, skip, out, xbc, state = refs[4:]
     step = pl.program_id(0)
-    rows = first_own.shape[2]
+    rows = first.shape[1]
     own = rows * 2
     past = xbc.shape[0] - TILE
 
@@ -42,14 +42,11 @@
         xbc[0:past] = xbc[TILE : TILE + past]
 
     gates = []
-    halves = ((first_own, first_other), (second_own, second_other))
+    own_half = second_own[0].astype(jnp.float32)
+    other_half = second_other[0].astype(jnp.float32)
     for core in range(2):
-        for half, (mine, other) in enumerate(halves):
-            block = jnp.where(
-                parity[0] == core,
-                mine[0, 0].astype(jnp.float32),
-                other[0, 0].astype(jnp.float32),
-            )
+        second = jnp.where(parity[0] == core, own_half, other_half)
+        for half, block in enumerate((first[core].astype(jnp.float32), second)):
             start = past + core * own + half * rows
             xbc[start : start + rows, :SLOT] = block[:, :SLOT]
             xbc[start : start + rows, SLOT:] = block[:, 2 * SLOT :]
@@ -118,18 +115,18 @@
 
 
 def scan(parity, projected, taps, conv_bias, head_rows, skip, width):
-    _, _, rows, columns = projected[0].shape
+    first, second_own, second_other = projected
+    owners, rows, columns = first.shape
     own = rows * 2
     per_step = 2
-    owners = per_step * SIDE * SIDE
-    by_y = pl.BlockSpec((1, 1, rows, columns), lambda i: (i % SIDE, i // SIDE, 0, 0))
-    by_x = pl.BlockSpec((1, 1, rows, columns), lambda i: (i // SIDE, i % SIDE, 0, 0))
+    by_device = pl.BlockSpec((per_step, rows, columns), lambda i: (i, 0, 0))
+    by_chip = pl.BlockSpec((1, rows, columns), lambda i: (i, 0, 0))
     whole = lambda array: pl.BlockSpec(array.shape, lambda i: (0,) * array.ndim)
     constants = (taps, conv_bias, head_rows, skip)
     return pl.pallas_call(
         scan_kernel,
         grid=(owners // per_step,),
-        in_specs=[pl.BlockSpec(memory_space=pltpu.SMEM), by_y, by_y, by_x, by_x]
+        in_specs=[pl.BlockSpec(memory_space=pltpu.SMEM), by_device, by_chip, by_chip]
         + [whole(array) for array in constants],
         out_specs=pl.BlockSpec((per_step, own, width), lambda i: (i, 0, 0)),
         out_shape=jax.ShapeDtypeStruct((owners, own, width), jnp.bfloat16),
@@ -216,6 +213,10 @@
         [move(behind[:half], dx, dy), move(ahead[half:], -dx, -dy)], axis=0
     )
     return block, ahead, far, behind
+
+
+def nothing(array):
+    return jnp.minimum(jnp.abs(array[0, 0].astype(jnp.float32)), 0.0).astype(jnp.int32)
 
 
 def place(parts, position):
@@ -249,14 +250,16 @@
     chip_heads = 2 * width // HEAD
     turned = width - 3 * HEAD
     inner = norm_gain.shape[0]
-    group = me // (owners // GROUPS)
 
     at_x, at_y = me // (2 * SIDE), me // 2 % SIDE
     rows = num_rows // 2
-    column = place(line(own_rows[:rows], 1, 0), at_x)
+    first = lax.all_gather(own_rows[:rows], "seq").reshape(owners * rows, depth)
     row = place(line(own_rows[rows:], 0, 1), at_y)
-    first_parts = line(column, 0, 1)
     second_parts = line(row, 1, 0)
+    second_own = place(second_parts, at_x)
+    second_other = move(second_own, 0, 0, 1)
+    early = me + nothing(row)
+    late = me + nothing(second_parts[1])
 
     def turn(columns):
         return jnp.where(odd, jnp.roll(columns, -turned, axis=-1), columns)
@@ -264,13 +267,14 @@
     def pad(array, size):
         return jnp.pad(array, ((0, 0), (0, size - array.shape[-1])))
 
-    def heads_of(array):
+    def heads_of(array, me=late):
         chip = lax.dynamic_slice_in_dim(array, me // 2 * chip_heads, chip_heads, -1)
         return jnp.where(
             odd, jnp.concatenate([chip[..., 4:7], chip[..., 3:4]], axis=-1), chip[..., :4]
         )
 
-    def states_of(array, start):
+    def states_of(array, start, me=late):
+        group = me // (owners // GROUPS)
         first = lax.dynamic_slice_in_dim(array, start + group * STATE, STATE, -1)
         second = lax.dynamic_slice_in_dim(
             array, start + (GROUPS + group) * STATE, STATE, -1
@@ -278,19 +282,19 @@
         return first, second
 
     both = gather_rows(jnp.concatenate([turn(w_x), turn(w_z)], axis=1), "req")
-    w_b, w_c = states_of(w_bc, 0)
+    w_b, w_c = states_of(w_bc, 0, early)
     weights = jnp.concatenate(
         [
             pad(both[:, :width], SLOT),
             pad(both[:, width:], SLOT),
             pad(w_b, TILE),
-            pad(jnp.concatenate([w_c, heads_of(w_dt)], axis=1), TILE),
+            pad(jnp.concatenate([w_c, heads_of(w_dt, early)], axis=1), TILE),
         ],
         axis=1,
     )
 
     def channels_of(array):
-        x_part = turn(lax.dynamic_slice_in_dim(array, me * width, width, -1))
+        x_part = turn(lax.dynamic_slice_in_dim(array, late * width, width, -1))
         b_part, c_part = states_of(array, inner)
         return jnp.concatenate([pad(x_part, SLOT), pad(b_part, TILE), pad(c_part, TILE)], axis=1)
 
@@ -305,17 +309,12 @@
         (jnp.arange(owners) % 2 == 1)[:, None], jnp.roll(gains, -turned, axis=1), gains
     )
 
-    def project(parts, position):
-        blocks = [
-            jnp.dot(part, weights, preferred_element_type=jnp.float32).astype(jnp.bfloat16)
-            for part in parts
-        ]
-        return place(blocks, position).reshape(SIDE, SIDE, rows, -1)
-
-    projected = []
-    for parts, position in ((first_parts, at_y), (second_parts, at_x)):
-        projected.append(project(parts, position))
-        projected.append(project([move(part, 0, 0, 1) for part in parts], position))
+    projected = [
+        jnp.dot(part, weights, preferred_element_type=jnp.float32)
+        .astype(jnp.bfloat16)
+        .reshape(-1, rows, weights.shape[1])
+        for part in (first, second_own, second_other)
+    ]
     parity = (me % 2)[None]
     gated = scan(parity, projected, taps, bias, head_rows, skip, width)
     mine = lax.all_to_all(gated, "seq", split_axis=0, concat_axis=0, tiled=True)

time: 182 us -> 187 us (1.027)
  between operations: 1.25 us -> 15.7 us
  starting transfers between devices: 41.8 us -> 30.8 us
  local copies, waits for them, and re-layouts: 42.7 us -> 52.2 us
  matrix products: 31.9 us -> 23.5 us
  other arithmetic: 13.3 us -> 16.2 us
  waiting for transfers between devices: 30.5 us -> 27.7 us
    ppermute x24 -> x9, starting transfers between devices: 31.2 us -> 21.2 us  [move(): return lax.ppermute(block, 'seq', pairs)]
    dot_general x16 -> x3, matrix products: 31.9 us -> 23.5 us  [local(): jnp.dot(part, weights, preferred_element_type=jnp.float32)]
    ppermute x4, waiting for transfers between devices: 3.87 us -> 0.01 us  [around(): lax.ppermute(block, axis, [(i, (i + distance) % size) for i in range(size)])]
    broadcast_in_dim x0 -> x2, local copies, waits for them, and re-layouts: none -> 3.01 us  [place(): whole = jnp.zeros((SIDE * rows,) + parts[0].shape[1:], parts[0].dtype)]
    dynamic_update_slice x6, local copies, waits for them, and re-layouts: 7.98 us -> 10.6 us  [place(): lax.dynamic_update_slice(whole, part, ((position + distance) % SIDE * row...]
    concatenate x1, other arithmetic: 0.49 us -> 3.06 us  [local(): jnp.concatenate([pad(both[:, :width], SLOT), pad(both[:, width:], SLOT),...]
    slice x1 -> x3, local copies, waits for them, and re-layouts: 1.9 us -> 4.34 us  [the longest x2 2.45 us: nothing(): array[0, 0].astype(jnp.float32)]
    another operation x7 -> x1, local copies, waits for them, and re-layouts: 2.98 us -> 0.77 us
  transfers between devices with their start and end apart: 29 -> 15, of which waited for: 4 -> 5; matrix products, arithmetic and copies ran while one was open for 46% -> 42% of each run, Pallas kernels for 0% -> 0%
where the time goes in v4:
time: 187 us; the launch traced here: 185 us
  local copies, waits for them, and re-layouts  52.2 us (28%)
  starting transfers between devices  30.8 us (16%)
  waiting for transfers between devices  27.7 us (15%)
  matrix products  23.5 us (13%)
  Pallas kernels  18.5 us (10%)
  other arithmetic  16.2 us (9%)
  between operations  15.7 us (8%)
    dot_general x3, matrix products, local(): jnp.dot(part, weights, preferred_element_type=jnp.float32)  23.5 us
    ppermute x9, starting transfers between devices, move(): return lax.ppermute(block, 'seq', pairs)  21.2 us
    pallas_call x1, Pallas kernels, scan(): pl.pallas_call(scan_kernel, grid=(owners // per_step,), in_specs=[pl.Bloc...  15.7 us
    all_to_all x1, waiting for transfers between devices, local(): mine = lax.all_to_all(gated, 'seq', split_axis=0, concat_axis=0, tiled=True)  15.4 us
    ppermute x9, waiting for transfers between devices, move(): return lax.ppermute(block, 'seq', pairs)  12.4 us
    dynamic_update_slice x6, local copies, waits for them, and re-layouts, place(): lax.dynamic_update_slice(whole, part, ((position + distance) % SIDE * row...  10.6 us
    ppermute x4, starting transfers between devices, around(): lax.ppermute(block, axis, [(i, (i + distance) % size) for i in range(size)])  5.87 us
    unnamed x22, local copies, waits for them, and re-layouts  5.81 us
  transfers between devices with their start and end apart: 15, of which 5 were waited for; matrix products, arithmetic and copies ran while one was open for 42% of the time, Pallas kernels for 0%

profile of v4, /device:TPU:1, one launch (start us, length us, event | category | flops | bytes accessed | tf_op | source)
XLA Modules:
  0.0 184.7 jit_solution(4273657335340180015)
XLA Ops:
  8.4 3.6 %collective-permute-start.4 = (bf16[32,3584]{1,0:T(8,128)(2,1)}, bf16[32,3584]{1,0:T(8,128)(2,1)}, u32[]{:S(2)}, u32[]{:S(2)}) collective-permute-start(bf16[32,3584]{1,0:T(8,128)(2,1)} %get-tuple-element.10), channel_id=1, source_target_pairs={{0,6},{1,7},{2,0},{3,1},{4,2},{5,3},{6,4},{7,5},{8,14},{9,15},{10,... | collective-permute-start | bytes 688136 | tf_op jit(solution)/shard_map/ppermute | solution.py:206
  18.9 2.1 %collective-permute-start.1 = (bf16[896,448]{0,1:T(8,128)(2,1)}, bf16[896,448]{0,1:T(8,128)(2,1)}, u32[]{:S(2)}, u32[]{:S(2)}) collective-permute-start(bf16[896,448]{0,1:T(8,128)(2,1)} %get-tuple-element.7), channel_id=1, source_target_pairs={{0,96},{32,0},{64,32},{96,64},{1,97},{33,1},{65,33},{97,65},{2,98}... | collective-permute-start | bytes 2408456 | tf_op jit(solution)/shard_map/ppermute | solution.py:182
  24.6 2.7 %collective-permute-start.7 = (bf16[16,3584]{1,0:T(8,128)(2,1)S(1)}, bf16[16,3584]{1,0:T(8,128)(2,1)S(1)}, u32[]{:S(2)}, u32[]{:S(2)}) collective-permute-start(bf16[16,3584]{1,0:T(8,128)(2,1)S(1)} %slice.155), channel_id=1, source_target_pairs={{0,6},{1,7},{2,0},{3,1},{4,2},{5,3},{6,4},{7,5},{8,14},{9,15},{10,... | collective-permute-start | bytes 344072 | tf_op jit(solution)/shard_map/ppermute | solution.py:206
  29.9 3.8 %collective-permute-done.6 = bf16[16,3584]{1,0:T(8,128)(2,1)S(1)} collective-permute-done((bf16[16,3584]{1,0:T(8,128)(2,1)S(1)}, bf16[16,3584]{1,0:T(8,128)(2,1)S(1)}, u32[]{:S(2)}, u32[]{:S(2)}) %collective-permute-start.6) | collective-permute-done | bytes 114720 | tf_op jit(solution)/shard_map/ppermute | solution.py:206
  42.7 3.2 %constant_dynamic-slice_fusion.8 = (bf16[3584,64]{1,0:T(8,128)(2,1)}, bf16[3584,64]{1,0:T(8,128)(2,1)S(1)}) fusion(bf16[3584,256]{1,0:T(8,128)(2,1)} %param.15, s32[]{:T(128)S(6)} %select_n.237, s32[]{:T(128)S(6)} %select_n.238), kind=kLoop, calls=%fused_computation.49 | loop fusion | bytes 1835016 | tf_op jit(solution)/shard_map/dynamic_slice | solution.py:278
  49.3 2.1 %collective-permute-start.3 = (bf16[448,448]{0,1:T(8,128)(2,1)}, bf16[448,448]{0,1:T(8,128)(2,1)}, u32[]{:S(2)}, u32[]{:S(2)}) collective-permute-start(bf16[448,448]{0,1:T(8,128)(2,1)} %slice.151), channel_id=1, source_target_pairs={{0,96},{32,0},{64,32},{96,64},{1,97},{33,1},{65,33},{97,65},{2,98}... | collective-permute-start | bytes 1204232 | tf_op jit(solution)/shard_map/ppermute | solution.py:182
  53.3 2.0 %broadcast_in_dim.31 = bf16[512,3584]{1,0:T(8,128)(2,1)} broadcast(bf16[]{:T(256)} %constant.171.clone.1), dimensions={} | broadcast | bytes 3670018 | tf_op jit(solution)/shard_map/broadcast_in_dim | solution.py:224
  55.3 2.2 %constant_dynamic-update-slice_fusion.2 = bf16[512,3584]{1,0:T(8,128)(2,1)} fusion(bf16[512,3584]{1,0:T(8,128)(2,1)} %broadcast_in_dim.31, bf16[128,3584]{1,0:T(8,128)(2,1)} %constant_dynamic-update-slice_fusion.3, s32[]{:T(128)S(6)} %select_n.245), kind=kLoop, calls=%fused_computation.47 | loop fusion | bytes 1835012 | tf_op jit(solution)/shard_map/dynamic_update_slice | solution.py:226
  57.5 2.4 %copy.22 = bf16[3584,68]{0,1:T(8,128)(2,1)} copy(bf16[3584,68]{1,0:T(8,128)(2,1)} %pad_maximum_fusion) | data formatting | bytes 974848
  60.0 2.4 %copy.21 = bf16[3584,64]{0,1:T(8,128)(2,1)} copy(bf16[3584,64]{1,0:T(8,128)(2,1)} %get-tuple-element.5) | data formatting | bytes 917504
  68.0 2.8 %collective-permute-start.11 = (bf16[64,3584]{1,0:T(8,128)(2,1)S(1)}, bf16[64,3584]{1,0:T(8,128)(2,1)S(1)}, u32[]{:S(2)}, u32[]{:S(2)}) collective-permute-start(bf16[64,3584]{1,0:T(8,128)(2,1)S(1)} %slice.158), channel_id=1, source_target_pairs={{0,24},{1,25},{2,26},{3,27},{4,28},{5,29},{6,30},{7,31},{8,0},{9,1... | collective-permute-start | bytes 1376264 | tf_op jit(solution)/shard_map/ppermute | solution.py:206
  71.9 2.2 %constant_dynamic-update-slice_fusion.1 = bf16[512,3584]{1,0:T(8,128)(2,1)} fusion(bf16[512,3584]{1,0:T(8,128)(2,1)} %constant_dynamic-update-slice_fusion.2, bf16[128,3584]{1,0:T(8,128)(2,1)} %collective-permute-done.8, s32[]{:T(128)S(6)} %select_n.247), kind=kLoop, calls=%fused_computation.46 | loop fusion | bytes 1835012 | tf_op jit(solution)/shard_map/dynamic_update_slice | solution.py:226
  74.1 5.1 %collective-permute-done.11 = bf16[64,3584]{1,0:T(8,128)(2,1)S(1)} collective-permute-done((bf16[64,3584]{1,0:T(8,128)(2,1)S(1)}, bf16[64,3584]{1,0:T(8,128)(2,1)S(1)}, u32[]{:S(2)}, u32[]{:S(2)}) %collective-permute-start.11) | collective-permute-done | bytes 458784 | tf_op jit(solution)/shard_map/ppermute | solution.py:206
  79.2 2.5 %collective-permute-done.10 = bf16[64,3584]{1,0:T(8,128)(2,1)S(1)} collective-permute-done((bf16[64,3584]{1,0:T(8,128)(2,1)S(1)}, bf16[64,3584]{1,0:T(8,128)(2,1)S(1)}, u32[]{:S(2)}, u32[]{:S(2)}) %collective-permute-start.10) | collective-permute-done | bytes 458784 | tf_op jit(solution)/shard_map/ppermute | solution.py:206
  82.7 2.2 %constant_dynamic-update-slice_fusion = bf16[512,3584]{1,0:T(8,128)(2,1)} fusion(bf16[512,3584]{1,0:T(8,128)(2,1)} %maximum_dynamic-update-slice_fusion, bf16[128,3584]{1,0:T(8,128)(2,1)} %collective-permute-done.9, s32[]{:T(128)S(6)} %select_n.251), kind=kLoop, calls=%fused_computation.45 | loop fusion | bytes 1835012 | tf_op jit(solution)/shard_map/dynamic_update_slice | solution.py:226
  84.8 10.4 %collective-permute-start.12 = (bf16[512,3584]{1,0:T(8,128)(2,1)}, bf16[512,3584]{1,0:T(8,128)(2,1)}, u32[]{:S(2)}, u32[]{:S(2)}) collective-permute-start(bf16[512,3584]{1,0:T(8,128)(2,1)} %constant_dynamic-update-slice_fusion), channel_id=1, source_target_pairs={{0,1},{1,0},{2,3},{3,2},{4,5},{5,4},{6,7},{7,6},{8,9},{9,8},{10,11... | collective-permute-start | bytes 11010056 | tf_op jit(solution)/shard_map/ppermute | solution.py:206
  95.3 3.1 %fusion.6 = bf16[3584,768]{0,1:T(8,128)(2,1)} fusion(bf16[3584,68]{0,1:T(8,128)(2,1)S(1)} %copy-done.3, bf16[3584,64]{0,1:T(8,128)(2,1)S(1)} %copy-done.4, bf16[3584,224]{0,1:T(8,128)(2,1)S(1)} %slice.153, bf16[3584,256]{0,1:T(8,128)(2,1)S(1)} %slice_select_fusion), kind=kLoop, calls=%fused_computation.11 | loop fusion | flops 49545216 | bytes 9891840 | tf_op jit(solution)/shard_map/concatenate | solution.py:286
  112.6 7.7 %convolution_convert_fusion.2 = bf16[512,768]{1,0:T(8,128)(2,1)} fusion(bf16[512,3584]{1,0:T(8,128)(2,1)} %constant_dynamic-update-slice_fusion, bf16[3584,768]{0,1:T(8,128)(2,1)} %fusion.6), kind=kOutput, calls=%fused_computation.17 | convolution fusion | flops 2818965504 | bytes 9961472 | tf_op jit(solution)/shard_map/dot_general | solution.py:313
  120.3 6.0 %convolution_convert_fusion.1 = bf16[512,768]{1,0:T(8,128)(2,1)} fusion(bf16[512,3584]{1,0:T(8,128)(2,1)} %collective-permute-done.12, bf16[3584,768]{0,1:T(8,128)(2,1)S(1)} %copy-done), kind=kOutput, calls=%fused_computation.16 | convolution fusion | flops 2818965504 | bytes 9961472 | tf_op jit(solution)/shard_map/dot_general | solution.py:313
  126.3 9.8 %fusion.8 = bf16[1024,768]{0,1:T(8,128)(2,1)S(1)} fusion(bf16[3584,768]{0,1:T(8,128)(2,1)} %fusion.6, bf16[1024,3584]{1,0:T(8,128)(2,1)} %bitcast.41), kind=kOutput, calls=%fused_computation.15 | convolution fusion | flops 5637931008 | bytes 14417920 | tf_op jit(solution)/shard_map/dot_general | solution.py:313
  137.7 15.7 %mixer_scan.1 = bf16[32,64,224]{2,1,0:T(8,128)(2,1)} custom-call(s32[1]{0:T(128)} %bitcast.1.refs_0_, bf16[32,32,768]{2,1,0:T(8,128)(2,1)} %bitcast.34, bf16[16,32,768]{2,1,0:T(8,128)(2,1)} %bitcast.35, bf16[16,32,768]{2,1,0:T(8,128)(2,1)} %bitcast.36, f32[4,512]{1,0:T(4,128)} %select_maximum_fusion.refs_4_, f32[1,512]{1,0:T(1,128)} %fusion.12.refs_5_, ...), custom_call_target="tpu_custom_call" | custom-call | tf_op jit(solution)/shard_map/mixer_scan/pallas_call | solution.py:126
  153.4 3.7 %all-to-all-start = ((bf16[32,64,224]{2,1,0:T(8,128)(2,1)}), bf16[32,64,224]{2,1,0:T(8,128)(2,1)S(1)}, u32[]{:S(2)}, u32[]{:S(2)}) async-start(bf16[32,64,224]{2,1,0:T(8,128)(2,1)} %mixer_scan.1), calls=%async_computation | async-start | bytes 2097152 | tf_op jit(solution)/shard_map/all_to_all | solution.py:320
  158.7 15.4 %all-to-all-done.gated = bf16[32,64,224]{2,1,0:T(8,128)(2,1)S(1)} async-done(((bf16[32,64,224]{2,1,0:T(8,128)(2,1)}), bf16[32,64,224]{2,1,0:T(8,128)(2,1)S(1)}, u32[]{:S(2)}, u32[]{:S(2)}) %all-to-all-start) | async-done | bytes 917536 | tf_op jit(solution)/shard_map/all_to_all | solution.py:320
  175.0 2.8 %gated_norm.1 = bf16[64,7168]{1,0:T(8,128)(2,1)} custom-call(s32[1]{0:T(128)S(6)} %sub.29.limit, bf16[32,64,224]{2,1,0:T(8,128)(2,1)} %copy-done.1, f32[32,224]{1,0:T(8,128)} %maximum_select_fusion.2.gain), custom_call_target="tpu_custom_call" | custom-call | tf_op jit(solution)/shard_map/gated_norm/pallas_call | solution.py:167
  (103 shorter events, 53.1 us)
Async XLA Ops:
  6.5 119.8 %all-gather.2.cloned.1.call-start = ((), (), s32[]{:S(2)}) async-start(), calls=%async_computation.1 | async-start | bytes 7569408 | tf_op jit(solution)/shard_map/all_gather | solution.py:256
  8.4 15.2 %collective-permute-start.4 = (bf16[32,3584]{1,0:T(8,128)(2,1)}, bf16[32,3584]{1,0:T(8,128)(2,1)}, u32[]{:S(2)}, u32[]{:S(2)}) collective-permute-start(bf16[32,3584]{1,0:T(8,128)(2,1)} %get-tuple-element.10), channel_id=1, source_target_pairs={{0,6},{1,7},{2,0},{3,1},{4,2},{5,3},{6,4},{7,5},{8,14},{9,15},{10,... | collective-permute-start | bytes 688136 | tf_op jit(solution)/shard_map/ppermute | solution.py:206
  12.1 15.2 %collective-permute-start.5 = (bf16[32,3584]{1,0:T(8,128)(2,1)}, bf16[32,3584]{1,0:T(8,128)(2,1)S(1)}, u32[]{:S(2)}, u32[]{:S(2)}) collective-permute-start(bf16[32,3584]{1,0:T(8,128)(2,1)} %get-tuple-element.10), channel_id=1, source_target_pairs={{0,2},{1,3},{2,4},{3,5},{4,6},{5,7},{6,0},{7,1},{8,10},{9,11},{10,... | collective-permute-start | bytes 688136 | tf_op jit(solution)/shard_map/ppermute | solution.py:206
  17.3 34.2 %collective-permute-start = (bf16[896,448]{0,1:T(8,128)(2,1)}, bf16[896,448]{0,1:T(8,128)(2,1)}, u32[]{:S(2)}, u32[]{:S(2)}) collective-permute-start(bf16[896,448]{0,1:T(8,128)(2,1)} %get-tuple-element.7), channel_id=1, source_target_pairs={{0,32},{32,64},{64,96},{96,0},{1,33},{33,65},{65,97},{97,1},{2,34}... | collective-permute-start | bytes 2408456 | tf_op jit(solution)/shard_map/ppermute | solution.py:182
  18.9 28.4 %collective-permute-start.1 = (bf16[896,448]{0,1:T(8,128)(2,1)}, bf16[896,448]{0,1:T(8,128)(2,1)}, u32[]{:S(2)}, u32[]{:S(2)}) collective-permute-start(bf16[896,448]{0,1:T(8,128)(2,1)} %get-tuple-element.7), channel_id=1, source_target_pairs={{0,96},{32,0},{64,32},{96,64},{1,97},{33,1},{65,33},{97,65},{2,98}... | collective-permute-start | bytes 2408456 | tf_op jit(solution)/shard_map/ppermute | solution.py:182
  24.6 5.4 %collective-permute-start.7 = (bf16[16,3584]{1,0:T(8,128)(2,1)S(1)}, bf16[16,3584]{1,0:T(8,128)(2,1)S(1)}, u32[]{:S(2)}, u32[]{:S(2)}) collective-permute-start(bf16[16,3584]{1,0:T(8,128)(2,1)S(1)} %slice.155), channel_id=1, source_target_pairs={{0,6},{1,7},{2,0},{3,1},{4,2},{5,3},{6,4},{7,5},{8,14},{9,15},{10,... | collective-permute-start | bytes 344072 | tf_op jit(solution)/shard_map/ppermute | solution.py:206
  27.2 6.5 %collective-permute-start.6 = (bf16[16,3584]{1,0:T(8,128)(2,1)S(1)}, bf16[16,3584]{1,0:T(8,128)(2,1)S(1)}, u32[]{:S(2)}, u32[]{:S(2)}) collective-permute-start(bf16[16,3584]{1,0:T(8,128)(2,1)S(1)} %slice.154), channel_id=1, source_target_pairs={{0,2},{1,3},{2,4},{3,5},{4,6},{5,7},{6,0},{7,1},{8,10},{9,11},{10,... | collective-permute-start | bytes 344072 | tf_op jit(solution)/shard_map/ppermute | solution.py:206
  37.1 29.7 %collective-permute-start.8 = (bf16[128,3584]{1,0:T(8,128)(2,1)}, bf16[128,3584]{1,0:T(8,128)(2,1)}, u32[]{:S(2)}, u32[]{:S(2)}) collective-permute-start(bf16[128,3584]{1,0:T(8,128)(2,1)} %constant_dynamic-update-slice_fusion.3), channel_id=1, source_target_pairs={{0,24},{1,25},{2,26},{3,27},{4,28},{5,29},{6,30},{7,31},{8,0},{9,1... | collective-permute-start | bytes 2752520 | tf_op jit(solution)/shard_map/ppermute | solution.py:206
  38.5 32.2 %collective-permute-start.9 = (bf16[128,3584]{1,0:T(8,128)(2,1)}, bf16[128,3584]{1,0:T(8,128)(2,1)}, u32[]{:S(2)}, u32[]{:S(2)}) collective-permute-start(bf16[128,3584]{1,0:T(8,128)(2,1)} %constant_dynamic-update-slice_fusion.3), channel_id=1, source_target_pairs={{0,8},{1,9},{2,10},{3,11},{4,12},{5,13},{6,14},{7,15},{8,16},{9,17... | collective-permute-start | bytes 2752520 | tf_op jit(solution)/shard_map/ppermute | solution.py:206
  42.7 3.2 %copy-start.2 = (bf16[3584,4]{1,0:T(8,128)(2,1)S(1)}, bf16[3584,4]{1,0:T(8,128)(2,1)}, u32[]{:S(2)}) copy-start(bf16[3584,4]{1,0:T(8,128)(2,1)} %copy.17) | copy-start | bytes 86020
  49.3 15.6 %collective-permute-start.3 = (bf16[448,448]{0,1:T(8,128)(2,1)}, bf16[448,448]{0,1:T(8,128)(2,1)}, u32[]{:S(2)}, u32[]{:S(2)}) collective-permute-start(bf16[448,448]{0,1:T(8,128)(2,1)} %slice.151), channel_id=1, source_target_pairs={{0,96},{32,0},{64,32},{96,64},{1,97},{33,1},{65,33},{97,65},{2,98}... | collective-permute-start | bytes 1204232 | tf_op jit(solution)/shard_map/ppermute | solution.py:182
  53.3 11.7 %collective-permute-start.2 = (bf16[448,448]{0,1:T(8,128)(2,1)}, bf16[448,448]{0,1:T(8,128)(2,1)}, u32[]{:S(2)}, u32[]{:S(2)}) collective-permute-start(bf16[448,448]{0,1:T(8,128)(2,1)} %slice.150), channel_id=1, source_target_pairs={{0,32},{32,64},{64,96},{96,0},{1,33},{33,65},{65,97},{97,1},{2,34}... | collective-permute-start | bytes 1204232 | tf_op jit(solution)/shard_map/ppermute | solution.py:182
  63.7 2.9 %copy-start.6 = (pred[256]{0:T(512)(128)(4,1)S(1)}, pred[256]{0:T(512)(128)(4,1)}, u32[]{:S(2)}) copy-start(pred[256]{0:T(512)(128)(4,1)} %constant.170.clone.1) | copy-start | bytes 772
  66.8 28.5 %copy-start.3 = (bf16[3584,68]{0,1:T(8,128)(2,1)S(1)}, bf16[3584,68]{0,1:T(8,128)(2,1)}, u32[]{:S(2)}) copy-start(bf16[3584,68]{0,1:T(8,128)(2,1)} %copy.22) | copy-start | bytes 1462276
  66.8 28.5 %copy-start.4 = (bf16[3584,64]{0,1:T(8,128)(2,1)S(1)}, bf16[3584,64]{0,1:T(8,128)(2,1)}, u32[]{:S(2)}) copy-start(bf16[3584,64]{0,1:T(8,128)(2,1)} %copy.21) | copy-start | bytes 1376260
  68.0 11.2 %collective-permute-start.11 = (bf16[64,3584]{1,0:T(8,128)(2,1)S(1)}, bf16[64,3584]{1,0:T(8,128)(2,1)S(1)}, u32[]{:S(2)}, u32[]{:S(2)}) collective-permute-start(bf16[64,3584]{1,0:T(8,128)(2,1)S(1)} %slice.158), channel_id=1, source_target_pairs={{0,24},{1,25},{2,26},{3,27},{4,28},{5,29},{6,30},{7,31},{8,0},{9,1... | collective-permute-start | bytes 1376264 | tf_op jit(solution)/shard_map/ppermute | solution.py:206
  71.8 9.9 %collective-permute-start.10 = (bf16[64,3584]{1,0:T(8,128)(2,1)S(1)}, bf16[64,3584]{1,0:T(8,128)(2,1)S(1)}, u32[]{:S(2)}, u32[]{:S(2)}) collective-permute-start(bf16[64,3584]{1,0:T(8,128)(2,1)S(1)} %slice.157), channel_id=1, source_target_pairs={{0,8},{1,9},{2,10},{3,11},{4,12},{5,13},{6,14},{7,15},{8,16},{9,17... | collective-permute-start | bytes 1376264 | tf_op jit(solution)/shard_map/ppermute | solution.py:206
  84.8 15.4 %copy-start.7 = (f32[112]{0:T(128)S(1)}, f32[112]{0:T(128)}, u32[]{:S(2)}) copy-start(f32[112]{0:T(128)} %param.17) | copy-start | bytes 1348
  84.8 16.1 %copy-start.8 = (f32[112]{0:T(128)S(1)}, f32[112]{0:T(128)}, u32[]{:S(2)}) copy-start(f32[112]{0:T(128)} %param.18) | copy-start | bytes 1348
  84.8 16.9 %copy-start.9 = (f32[112]{0:T(128)S(1)}, f32[112]{0:T(128)}, u32[]{:S(2)}) copy-start(f32[112]{0:T(128)} %param.21) | copy-start | bytes 1348
  84.8 35.5 %collective-permute-start.12 = (bf16[512,3584]{1,0:T(8,128)(2,1)}, bf16[512,3584]{1,0:T(8,128)(2,1)}, u32[]{:S(2)}, u32[]{:S(2)}) collective-permute-start(bf16[512,3584]{1,0:T(8,128)(2,1)} %constant_dynamic-update-slice_fusion), channel_id=1, source_target_pairs={{0,1},{1,0},{2,3},{3,2},{4,5},{5,4},{6,7},{7,6},{8,9},{9,8},{10,11... | collective-permute-start | bytes 11010056 | tf_op jit(solution)/shard_map/ppermute | solution.py:206
  112.6 7.7 %copy-start = (bf16[3584,768]{0,1:T(8,128)(2,1)S(1)}, bf16[3584,768]{0,1:T(8,128)(2,1)}, u32[]{:S(2)}) copy-start(bf16[3584,768]{0,1:T(8,128)(2,1)} %fusion.6) | copy-start | bytes 16515076
  137.7 19.4 %copy-start.5 = (f32[7168]{0:T(1024)S(1)}, f32[7168]{0:T(1024)}, u32[]{:S(2)}) copy-start(f32[7168]{0:T(1024)} %param.22) | copy-start | bytes 86020
  153.4 20.6 %all-to-all-start = ((bf16[32,64,224]{2,1,0:T(8,128)(2,1)}), bf16[32,64,224]{2,1,0:T(8,128)(2,1)S(1)}, u32[]{:S(2)}, u32[]{:S(2)}) async-start(bf16[32,64,224]{2,1,0:T(8,128)(2,1)} %mixer_scan.1), calls=%async_computation | async-start | bytes 2097152 | tf_op jit(solution)/shard_map/all_to_all | solution.py:320
  (1 other events, 1.0 us)
Sparse Core Ops, SparseCore 0:
  9.6 66.7 all-gather.1

commit v5 on v2

--- a/solution.py
+++ b/solution.py
@@ -12,7 +12,6 @@
 HEAD = 64
 TILE = 128
 SLOT = 256
-PIECES = 1
 
 
 def split(value):
@@ -24,32 +23,30 @@
     return lax.dot_general(a, b, (dims, ((), ())), preferred_element_type=jnp.float32)
 
 
-def scan_kernel(*refs):
-    projected = refs[:PIECES]
-    taps, conv_bias, head_rows, skip, out, xbc, state = refs[PIECES:]
+def scan_kernel(
+    tokens, weights, taps, conv_bias, head_rows, skip, out, ahead, xbc, state, *, own
+):
     step = pl.program_id(0)
-    rows = projected[0].shape[1]
-    own = rows * PIECES
     past = xbc.shape[0] - TILE
 
     @pl.when(step == 0)
+    def _():
+        ahead[...] = jnp.zeros_like(ahead)
+
+    @pl.when(step <= 1)
     def _():
         xbc[...] = jnp.zeros_like(xbc)
         state[...] = jnp.zeros_like(state)
 
-    @pl.when(step > 0)
+    @pl.when(step > 1)
     def _():
         xbc[0:past] = xbc[TILE : TILE + past]
 
-    gates = []
-    for owner in range(TILE // own):
-        for piece in range(PIECES):
-            block = projected[piece][owner]
-            start = past + owner * own + piece * rows
-            xbc[start : start + rows, :SLOT] = block[:, :SLOT].astype(jnp.float32)
-            xbc[start : start + rows, SLOT:] = block[:, 2 * SLOT :].astype(jnp.float32)
-            gates.append(block[:, SLOT : 2 * SLOT])
-    gate = jnp.concatenate(gates, axis=0).astype(jnp.float32)
+    projected = ahead[...]
+    xbc[past : past + TILE, :SLOT] = projected[:, :SLOT].astype(jnp.float32)
+    xbc[past : past + TILE, SLOT:] = projected[:, 2 * SLOT :].astype(jnp.float32)
+    gate = projected[:, SLOT : 2 * SLOT].astype(jnp.float32)
+    ahead[...] = matmul(tokens[...], weights[...]).astype(jnp.bfloat16)
 
     total = conv_bias[...]
     count = taps.shape[0]
@@ -112,25 +109,26 @@
         state[:, span] = jnp.exp(last) * before[:, span] + block
 
 
-def scan(projected, taps, conv_bias, head_rows, skip, width):
-    owners, rows, columns = projected[0].shape
-    own = rows * PIECES
+def scan(tokens, weights, taps, conv_bias, head_rows, skip, own, width):
+    positions, depth = tokens.shape
+    steps = positions // TILE
     per_step = TILE // own
     whole = lambda array: pl.BlockSpec(array.shape, lambda i: (0,) * array.ndim)
-    constants = (taps, conv_bias, head_rows, skip)
+    constants = (weights, taps, conv_bias, head_rows, skip)
     return pl.pallas_call(
-        scan_kernel,
-        grid=(owners // per_step,),
-        in_specs=[pl.BlockSpec((per_step, rows, columns), lambda i: (i, 0, 0))] * PIECES
+        functools.partial(scan_kernel, own=own),
+        grid=(steps + 1,),
+        in_specs=[pl.BlockSpec((TILE, depth), lambda i: (jnp.minimum(i, steps - 1), 0))]
         + [whole(array) for array in constants],
-        out_specs=pl.BlockSpec((per_step, own, width), lambda i: (i, 0, 0)),
-        out_shape=jax.ShapeDtypeStruct((owners, own, width), jnp.bfloat16),
+        out_specs=pl.BlockSpec((per_step, own, width), lambda i: (jnp.maximum(i - 1, 0), 0, 0)),
+        out_shape=jax.ShapeDtypeStruct((positions // own, own, width), jnp.bfloat16),
         scratch_shapes=[
+            pltpu.VMEM((TILE, weights.shape[1]), jnp.bfloat16),
             pltpu.VMEM((TILE + 8, 2 * SLOT), jnp.float32),
             pltpu.VMEM((TILE, SLOT), jnp.float32),
         ],
         name="mixer_scan",
-    )(*projected, *constants)
+    )(tokens, *constants)
 
 
 def norm_kernel(turned, limit, gated, gain, out):
@@ -216,10 +214,7 @@
     inner = norm_gain.shape[0]
     group = me // (owners // GROUPS)
 
-    rows = num_rows // PIECES
-    token_pieces = [
-        lax.all_gather(own_rows[j * rows : (j + 1) * rows], "seq") for j in range(PIECES)
-    ]
+    gathered = lax.all_gather(own_rows, "seq").reshape(owners * num_rows, depth)
 
     def turn(columns):
         return jnp.where(odd, jnp.roll(columns, -turned, axis=-1), columns)
@@ -268,13 +263,7 @@
         (jnp.arange(owners) % 2 == 1)[:, None], jnp.roll(gains, -turned, axis=1), gains
     )
 
-    projected = []
-    for piece in token_pieces:
-        block = jnp.dot(
-            piece.reshape(owners * rows, depth), weights, preferred_element_type=jnp.float32
-        ).astype(jnp.bfloat16)
-        projected.append(block.reshape(owners, rows, -1))
-    gated = scan(projected, taps, bias, head_rows, skip, width)
+    gated = scan(gathered, weights, taps, bias, head_rows, skip, num_rows, width)
     mine = lax.all_to_all(gated, "seq", split_axis=0, concat_axis=0, tiled=True)
     limit = lengths - me * num_rows
     return norm(limit, mine, gains, turned)[None]

time: 155 us -> 142 us (0.916)
  matrix products: 21.4 us -> 0 us
  Pallas kernels: 18.5 us -> 30.1 us
  other arithmetic: 12.6 us -> 20.6 us
  local copies, waits for them, and re-layouts: 33.5 us -> 27.4 us
  waiting for transfers between devices: 41 us -> 36 us
    dot_general x1 -> x0, matrix products: 21.4 us -> none  [local(): jnp.dot(piece.reshape(owners * rows, depth), weights, preferred_element_t...]
    pallas_call x1, Pallas kernels: 15.7 us -> 27.3 us  [scan(): pl.pallas_call(functools.partial(scan_kernel, own=own), grid=(steps + 1,)...]
    all_gather x1, waiting for transfers between devices: 24.8 us -> 16.8 us  [local(): gathered = lax.all_gather(own_rows, 'seq').reshape(owners * num_rows, depth)]
    slice x7, local copies, waits for them, and re-layouts: 5.26 us -> 2.05 us  [turn(): return jnp.where(odd, jnp.roll(columns, -turned, axis=-1), columns)]
    concatenate x0 -> x1, other arithmetic: none -> 3.2 us  [local(): jnp.concatenate([pad(both[:, :width], SLOT), pad(both[:, width:], SLOT),...]
    ppermute x4, waiting for transfers between devices: 0.01 us -> 3.06 us  [around(): lax.ppermute(block, axis, [(i, (i + distance) % size) for i in range(size)])]
    convert_element_type x1 -> x0, local copies, waits for them, and re-layouts: 2.83 us -> none  [local(): block = jnp.dot(piece.reshape(owners * rows, depth), weights, preferred_e...]
    unnamed x16, local copies, waits for them, and re-layouts: 5.87 us -> 3.42 us
  transfers between devices with their start and end apart: 6 -> 6, of which waited for: 2 -> 3; matrix products, arithmetic and copies ran while one was open for 27% -> 33% of each run, Pallas kernels for 0% -> 0%
where the time goes in v5:
time: 142 us; the launch traced here: 141 us
  waiting for transfers between devices  36 us (25%)
  Pallas kernels  30.1 us (21%)
  local copies, waits for them, and re-layouts  27.4 us (19%)
  other arithmetic  20.6 us (15%)
  between operations  14.3 us (10%)
  starting transfers between devices  12.9 us (9%)
    pallas_call x1, Pallas kernels, scan(): pl.pallas_call(functools.partial(scan_kernel, own=own), grid=(steps + 1,)...  27.3 us
    all_gather x1, waiting for transfers between devices, local(): gathered = lax.all_gather(own_rows, 'seq').reshape(owners * num_rows, depth)  16.8 us
    all_to_all x1, waiting for transfers between devices, local(): mine = lax.all_to_all(gated, 'seq', split_axis=0, concat_axis=0, tiled=True)  15.4 us
    ppermute x4, starting transfers between devices, around(): lax.ppermute(block, axis, [(i, (i + distance) % size) for i in range(size)])  7.5 us
    all_to_all x1, starting transfers between devices, local(): mine = lax.all_to_all(gated, 'seq', split_axis=0, concat_axis=0, tiled=True)  5.41 us
    unnamed x16, local copies, waits for them, and re-layouts  3.42 us
    another operation x2, other arithmetic, local(): jnp.stack([heads_of(dt_bias), heads_of(a_rate)])  3.23 us
    concatenate x1, other arithmetic, local(): jnp.concatenate([pad(both[:, :width], SLOT), pad(both[:, width:], SLOT),...  3.2 us
  transfers between devices with their start and end apart: 6, of which 3 were waited for; matrix products, arithmetic and copies ran while one was open for 33% of the time, Pallas kernels for 0%

profile of v5, /device:TPU:1, one launch (start us, length us, event | category | flops | bytes accessed | tf_op | source)
XLA Modules:
  0.0 141.3 jit_solution(4800751576421023879)
XLA Ops:
  8.7 1.2 copy.41
  10.6 2.0 %broadcast_in_dim.19 = bf16[3584,448]{1,0:T(8,128)(2,1)} broadcast(bf16[]{:T(256)} %constant.92.clone.1), dimensions={} | broadcast | bytes 3211266 | tf_op jit(solution)/shard_map/broadcast_in_dim | solution.py:186
  12.7 1.3 pad_maximum_fusion
  14.8 2.5 %collective-permute-start = (bf16[896,448]{0,1:T(8,128)(2,1)S(1)}, bf16[896,448]{0,1:T(8,128)(2,1)}, u32[]{:S(2)}, u32[]{:S(2)}) collective-permute-start(bf16[896,448]{0,1:T(8,128)(2,1)S(1)} %copy.44), channel_id=1, source_target_pairs={{0,32},{32,64},{64,96},{96,0},{1,33},{33,65},{65,97},{97,1},{2,34}... | collective-permute-start | bytes 2408456 | tf_op jit(solution)/shard_map/ppermute | solution.py:175
  17.3 2.2 %collective-permute-start.1 = (bf16[896,448]{0,1:T(8,128)(2,1)S(1)}, bf16[896,448]{0,1:T(8,128)(2,1)S(1)}, u32[]{:S(2)}, u32[]{:S(2)}) collective-permute-start(bf16[896,448]{0,1:T(8,128)(2,1)S(1)} %copy.44), channel_id=1, source_target_pairs={{0,96},{32,0},{64,32},{96,64},{1,97},{33,1},{65,33},{97,65},{2,98}... | collective-permute-start | bytes 2408456 | tf_op jit(solution)/shard_map/ppermute | solution.py:175
  28.3 1.3 constant_dynamic-slice_fusion.5
  30.4 1.4 maximum_select_fusion.3
  32.9 2.0 %constant_dynamic-slice_fusion.6 = (bf16[3584,64]{1,0:T(8,128)(2,1)S(1)}, bf16[3584,64]{1,0:T(8,128)(2,1)S(1)}) fusion(bf16[3584,256]{1,0:T(8,128)(2,1)} %param.15, s32[]{:T(128)S(6)} %select_n.152, s32[]{:T(128)S(6)} %select_n.151), kind=kLoop, calls=%fused_computation.39 | loop fusion | bytes 1835016 | tf_op jit(solution)/shard_map/dynamic_slice | solution.py:233
  35.5 1.9 %fusion.13 = (f32[1,4]{1,0:T(1,128)}, f32[1,4]{1,0:T(1,128)}) fusion(pred[]{:T(512)S(6)} %eq.19, f32[1]{0:T(128)} %slice.103, f32[3]{0:T(128)S(1)} %slice.102, f32[7]{0:T(128)S(1)} %dynamic_slice.45, f32[7]{0:T(128)S(1)} %dynamic_slice.46, f32[1]{0:T(128)} %slice.106, f32[3]{0:T(128)S(1)} %slice.105), kind=kLoop, calls=%fused_computation.53 | loop fusion | flops 16 | bytes 97 | tf_op jit(solution)/shard_map/stack | solution.py:258
  37.4 1.5 %fusion.9 = bf16[3584,128]{1,0:T(8,128)(2,1)} fusion(bf16[3584,4]{1,0:T(8,128)(2,1)S(1)} %copy.54, bf16[3584,64]{1,0:T(8,128)(2,1)S(1)} %get-tuple-element.5), kind=kLoop, calls=%fused_computation.15 | loop fusion | flops 3211264 | bytes 1404928 | tf_op jit(solution)/shard_map/concatenate | solution.py:245
  39.0 1.5 %copy.45 = bf16[896,448]{1,0:T(8,128)(2,1)S(1)} copy(bf16[896,448]{0,1:T(8,128)(2,1)} %collective-permute-done) | data formatting | bytes 1605632 | tf_op jit(solution)/shard_map/ppermute | solution.py:175
  42.1 2.7 %collective-permute-start.3 = (bf16[448,448]{1,0:T(8,128)(2,1)S(1)}, bf16[448,448]{1,0:T(8,128)(2,1)}, u32[]{:S(2)}, u32[]{:S(2)}) collective-permute-start(bf16[448,448]{1,0:T(8,128)(2,1)S(1)} %slice.118), channel_id=1, source_target_pairs={{0,96},{32,0},{64,32},{96,64},{1,97},{33,1},{65,33},{97,65},{2,98}... | collective-permute-start | bytes 1204232 | tf_op jit(solution)/shard_map/ppermute | solution.py:175
  44.8 1.3 select_maximum_fusion.2.head_rows
  47.5 1.3 select_maximum_fusion.taps
  50.8 3.1 %collective-permute-done.2 = bf16[448,448]{1,0:T(8,128)(2,1)} collective-permute-done((bf16[448,448]{1,0:T(8,128)(2,1)}, bf16[448,448]{1,0:T(8,128)(2,1)}, u32[]{:S(2)}, u32[]{:S(2)}) %collective-permute-start.2) | collective-permute-done | bytes 401440 | tf_op jit(solution)/shard_map/ppermute | solution.py:175
  53.9 2.2 %maximum_dynamic-update-slice_fusion = bf16[3584,448]{1,0:T(8,128)(2,1)} fusion(bf16[3584,448]{1,0:T(8,128)(2,1)} %constant_dynamic-update-slice_fusion, s32[]{:T(128)S(6)} %select_n.149, bf16[448,448]{1,0:T(8,128)(2,1)} %collective-permute-done.3, bf16[448,448]{1,0:T(8,128)(2,1)} %collective-permute-done.2), kind=kLoop, calls=%fused_computation.17 | loop fusion | flops 1605632 | bytes 1835012 | tf_op jit(solution)/shard_map/dynamic_update_slice | solution.py:188
  56.1 3.0 %slice.120 = bf16[3584,224]{1,0:T(8,128)(2,1)S(1)} slice(bf16[3584,448]{1,0:T(8,128)(2,1)} %maximum_dynamic-update-slice_fusion), slice={[0:3584], [224:448]} | slice | bytes 3211264 | tf_op jit(solution)/shard_map/slice | solution.py:243
  59.1 1.9 %slice_select_fusion = bf16[3584,256]{1,0:T(8,128)(2,1)S(1)} fusion(bf16[3584,448]{1,0:T(8,128)(2,1)} %maximum_dynamic-update-slice_fusion, pred[256]{0:T(512)(128)(4,1)S(1)} %copy-done.3), kind=kLoop, calls=%fused_computation.14 | loop fusion | flops 917504 | bytes 3670272 | tf_op jit(solution)/shard_map/jit(_pad)/pad | solution.py:223
  61.0 3.2 %fusion.5.weights = bf16[3584,768]{1,0:T(8,128)(2,1)} fusion(bf16[3584,64]{1,0:T(8,128)(2,1)S(1)} %get-tuple-element.6, bf16[3584,224]{1,0:T(8,128)(2,1)S(1)} %slice.120, bf16[3584,128]{1,0:T(8,128)(2,1)S(1)} %copy-done.1, bf16[3584,256]{1,0:T(8,128)(2,1)S(1)} %slice_select_fusion), kind=kLoop, calls=%fused_computation.9 | loop fusion | flops 44040192 | bytes 10321920 | tf_op jit(solution)/shard_map/concatenate | solution.py:240
  64.2 16.8 %all-gather.2.cloned.1.call-done = bf16[32,64,3584]{2,1,0:T(8,128)(2,1)} async-done(((bf16[1,64,3584]{2,1,0:T(8,128)(2,1)}), bf16[32,64,3584]{2,1,0:T(8,128)(2,1)}) %all-gather.2.cloned.1.call-update) | async-done | bytes 14680080 | tf_op jit(solution)/shard_map/all_gather | solution.py:217
  81.0 27.3 %mixer_scan.1 = bf16[32,64,224]{2,1,0:T(8,128)(2,1)} custom-call(bf16[2048,3584]{1,0:T(8,128)(2,1)} %bitcast.16, bf16[3584,768]{1,0:T(8,128)(2,1)} %fusion.5.weights, f32[4,512]{1,0:T(4,128)} %select_maximum_fusion.taps, f32[1,512]{1,0:T(1,128)} %fusion.12.conv_bias, f32[2,128]{1,0:T(2,128)} %select_maximum_fusion.2.head_rows, ...), custom_call_target="tpu_custom_call" | custom-call | tf_op jit(solution)/shard_map/mixer_scan/pallas_call | solution.py:118
  108.3 5.4 %all-to-all-start = ((bf16[32,64,224]{2,1,0:T(8,128)(2,1)}), bf16[32,64,224]{2,1,0:T(8,128)(2,1)S(1)}, u32[]{:S(2)}, u32[]{:S(2)}) async-start(bf16[32,64,224]{2,1,0:T(8,128)(2,1)} %mixer_scan.1), calls=%async_computation | async-start | bytes 2097152 | tf_op jit(solution)/shard_map/all_to_all | solution.py:267
  115.3 15.4 %all-to-all-done.gated = bf16[32,64,224]{2,1,0:T(8,128)(2,1)S(1)} async-done(((bf16[32,64,224]{2,1,0:T(8,128)(2,1)}), bf16[32,64,224]{2,1,0:T(8,128)(2,1)S(1)}, u32[]{:S(2)}, u32[]{:S(2)}) %all-to-all-start) | async-done | bytes 917536 | tf_op jit(solution)/shard_map/all_to_all | solution.py:267
  131.7 2.8 %gated_norm.1 = bf16[64,7168]{1,0:T(8,128)(2,1)} custom-call(s32[1]{0:T(128)S(6)} %sub.17.limit, bf16[32,64,224]{2,1,0:T(8,128)(2,1)} %copy-done, f32[32,224]{1,0:T(8,128)} %maximum_select_fusion.2.gain), custom_call_target="tpu_custom_call" | custom-call | tf_op jit(solution)/shard_map/gated_norm/pallas_call | solution.py:160
  (61 shorter events, 21.6 us)
Async XLA Ops:
  6.5 74.5 %all-gather.2.cloned.1.call-start = ((), (), s32[]{:S(2)}) async-start(), calls=%async_computation.1 | async-start | bytes 15138816 | tf_op jit(solution)/shard_map/all_gather | solution.py:217
  10.6 8.9 %copy-start.4 = (f32[112]{0:T(128)S(1)}, f32[112]{0:T(128)}, u32[]{:S(2)}) copy-start(f32[112]{0:T(128)} %param.17) | copy-start | bytes 1348
  10.6 9.7 %copy-start.5 = (f32[112]{0:T(128)S(1)}, f32[112]{0:T(128)}, u32[]{:S(2)}) copy-start(f32[112]{0:T(128)} %param.18) | copy-start | bytes 1348
  10.6 10.4 %copy-start.6 = (f32[112]{0:T(128)S(1)}, f32[112]{0:T(128)}, u32[]{:S(2)}) copy-start(f32[112]{0:T(128)} %param.21) | copy-start | bytes 1348
  14.8 24.2 %collective-permute-start = (bf16[896,448]{0,1:T(8,128)(2,1)S(1)}, bf16[896,448]{0,1:T(8,128)(2,1)}, u32[]{:S(2)}, u32[]{:S(2)}) collective-permute-start(bf16[896,448]{0,1:T(8,128)(2,1)S(1)} %copy.44), channel_id=1, source_target_pairs={{0,32},{32,64},{64,96},{96,0},{1,33},{33,65},{65,97},{97,1},{2,34}... | collective-permute-start | bytes 2408456 | tf_op jit(solution)/shard_map/ppermute | solution.py:175
  17.3 24.0 %collective-permute-start.1 = (bf16[896,448]{0,1:T(8,128)(2,1)S(1)}, bf16[896,448]{0,1:T(8,128)(2,1)S(1)}, u32[]{:S(2)}, u32[]{:S(2)}) collective-permute-start(bf16[896,448]{0,1:T(8,128)(2,1)S(1)} %copy.44), channel_id=1, source_target_pairs={{0,96},{32,0},{64,32},{96,64},{1,97},{33,1},{65,33},{97,65},{2,98}... | collective-permute-start | bytes 2408456 | tf_op jit(solution)/shard_map/ppermute | solution.py:175
  41.3 12.6 %collective-permute-start.2 = (bf16[448,448]{1,0:T(8,128)(2,1)}, bf16[448,448]{1,0:T(8,128)(2,1)}, u32[]{:S(2)}, u32[]{:S(2)}) collective-permute-start(bf16[448,448]{1,0:T(8,128)(2,1)} %slice.117), channel_id=1, source_target_pairs={{0,32},{32,64},{64,96},{96,0},{1,33},{33,65},{65,97},{97,1},{2,34}... | collective-permute-start | bytes 1204232 | tf_op jit(solution)/shard_map/ppermute | solution.py:175
  42.1 11.8 %collective-permute-start.3 = (bf16[448,448]{1,0:T(8,128)(2,1)S(1)}, bf16[448,448]{1,0:T(8,128)(2,1)}, u32[]{:S(2)}, u32[]{:S(2)}) collective-permute-start(bf16[448,448]{1,0:T(8,128)(2,1)S(1)} %slice.118), channel_id=1, source_target_pairs={{0,96},{32,0},{64,32},{96,64},{1,97},{33,1},{65,33},{97,65},{2,98}... | collective-permute-start | bytes 1204232 | tf_op jit(solution)/shard_map/ppermute | solution.py:175
  49.8 9.3 %copy-start.3 = (pred[256]{0:T(512)(128)(4,1)S(1)}, pred[256]{0:T(512)(128)(4,1)}, u32[]{:S(2)}) copy-start(pred[256]{0:T(512)(128)(4,1)} %constant.91.clone.1) | copy-start | bytes 772
  56.1 4.9 %copy-start.1 = (bf16[3584,128]{1,0:T(8,128)(2,1)S(1)}, bf16[3584,128]{1,0:T(8,128)(2,1)}, u32[]{:S(2)}) copy-start(bf16[3584,128]{1,0:T(8,128)(2,1)} %fusion.9) | copy-start | bytes 2752516
  81.0 32.8 %copy-start.2 = (f32[7168]{0:T(1024)S(1)}, f32[7168]{0:T(1024)}, u32[]{:S(2)}) copy-start(f32[7168]{0:T(1024)} %param.22) | copy-start | bytes 86020
  108.3 22.3 %all-to-all-start = ((bf16[32,64,224]{2,1,0:T(8,128)(2,1)}), bf16[32,64,224]{2,1,0:T(8,128)(2,1)S(1)}, u32[]{:S(2)}, u32[]{:S(2)}) async-start(bf16[32,64,224]{2,1,0:T(8,128)(2,1)} %mixer_scan.1), calls=%async_computation | async-start | bytes 2097152 | tf_op jit(solution)/shard_map/all_to_all | solution.py:267
  130.7 1.0 copy-start
Sparse Core Ops, SparseCore 0:
  9.6 71.3 all-gather.1

commit v6 on v5

--- a/solution.py
+++ b/solution.py
@@ -11,6 +11,7 @@
 STATE = 64
 HEAD = 64
 TILE = 128
+AHEAD = 256
 SLOT = 256
 
 
@@ -38,92 +39,91 @@
         xbc[...] = jnp.zeros_like(xbc)
         state[...] = jnp.zeros_like(state)
 
-    @pl.when(step > 1)
-    def _():
+    every = ahead[...]
+    ahead[...] = matmul(tokens[...], weights[...]).astype(jnp.bfloat16)
+    for part in range(AHEAD // TILE):
         xbc[0:past] = xbc[TILE : TILE + past]
-
-    projected = ahead[...]
-    xbc[past : past + TILE, :SLOT] = projected[:, :SLOT].astype(jnp.float32)
-    xbc[past : past + TILE, SLOT:] = projected[:, 2 * SLOT :].astype(jnp.float32)
-    gate = projected[:, SLOT : 2 * SLOT].astype(jnp.float32)
-    ahead[...] = matmul(tokens[...], weights[...]).astype(jnp.bfloat16)
-
-    total = conv_bias[...]
-    count = taps.shape[0]
-    for k in range(count):
-        first = past - (count - 1) + k
-        total = total + taps[k : k + 1] * xbc[first : first + TILE]
-    conved = (total * jax.nn.sigmoid(total)).astype(jnp.bfloat16)
-    b_proj = conved[:, SLOT : SLOT + TILE]
-    c_proj = conved[:, SLOT + TILE :]
-
-    raw = xbc[past : past + TILE, SLOT + TILE :]
-    step_size = jax.nn.softplus(raw + head_rows[0:1])
-    log_decay = -step_size * head_rows[1:2]
-    row = lax.broadcasted_iota(jnp.int32, (TILE, TILE), 0)
-    lane = lax.broadcasted_iota(jnp.int32, (TILE, TILE), 1)
-    causal = row >= lane
-    running = jnp.dot(
-        causal.astype(jnp.float32),
-        log_decay,
-        precision=lax.Precision.HIGHEST,
-        preferred_element_type=jnp.float32,
-    )
-    running_rows = running.T
-    step_rows = step_size.T
-    affinity = jnp.where(causal, matmul(c_proj, b_proj, ((1,), (1,))), 0.0)
-    before = state[...]
-    before_high, before_low = split(before)
-    carried = matmul(c_proj, before_high) + matmul(c_proj, before_low)
-
-    left = lane < HEAD
-    for tile in range(SLOT // TILE):
-        span = slice(tile * TILE, (tile + 1) * TILE)
-        x = conved[:, span]
-        mixing, columns, steps = [], [], []
-        for half in range(2):
-            at = STATE + 2 * tile + half
-            column = jnp.broadcast_to(running[:, at : at + 1], (TILE, TILE))
-            decay = jnp.exp(jnp.minimum(column - running_rows[at : at + 1], 0.0))
-            mixing.append(decay * affinity * step_rows[at : at + 1])
-            columns.append(column)
-            steps.append(jnp.broadcast_to(step_size[:, at : at + 1], (TILE, TILE)))
-        weights, rest = split(jnp.concatenate(mixing, axis=1))
-        zero = jnp.zeros_like(x)
-        values = jnp.concatenate([jnp.where(left, x, zero), jnp.where(left, zero, x)], axis=0)
-        intra = matmul(weights, values) + matmul(rest, values)
-        run = jnp.where(left, columns[0], columns[1])
-        last = run[TILE - 1 :]
-        x32 = x.astype(jnp.float32)
-        result = intra + jnp.exp(run) * carried[:, span] + skip[:, span] * x32
-        z = gate[:, span]
-        gated = (result * (z * jax.nn.sigmoid(z))).astype(jnp.bfloat16)
-        width = min(out.shape[2] - tile * TILE, TILE)
-        for owner in range(TILE // own):
-            out[owner, :, tile * TILE : tile * TILE + width] = gated[
-                owner * own : (owner + 1) * own, :width
-            ]
-        added = x32 * (jnp.exp(last - run) * jnp.where(left, steps[0], steps[1]))
-        added_high, added_low = split(added)
-        block = matmul(b_proj, added_high, ((0,), (0,))) + matmul(b_proj, added_low, ((0,), (0,)))
-        state[:, span] = jnp.exp(last) * before[:, span] + block
+        projected = every[part * TILE : (part + 1) * TILE]
+        xbc[past : past + TILE, :SLOT] = projected[:, :SLOT].astype(jnp.float32)
+        xbc[past : past + TILE, SLOT:] = projected[:, 2 * SLOT :].astype(jnp.float32)
+        gate = projected[:, SLOT : 2 * SLOT].astype(jnp.float32)
+
+        total = conv_bias[...]
+        count = taps.shape[0]
+        for k in range(count):
+            first = past - (count - 1) + k
+            total = total + taps[k : k + 1] * xbc[first : first + TILE]
+        conved = (total * jax.nn.sigmoid(total)).astype(jnp.bfloat16)
+        b_proj = conved[:, SLOT : SLOT + TILE]
+        c_proj = conved[:, SLOT + TILE :]
+
+        raw = xbc[past : past + TILE, SLOT + TILE :]
+        step_size = jax.nn.softplus(raw + head_rows[0:1])
+        log_decay = -step_size * head_rows[1:2]
+        row = lax.broadcasted_iota(jnp.int32, (TILE, TILE), 0)
+        lane = lax.broadcasted_iota(jnp.int32, (TILE, TILE), 1)
+        causal = row >= lane
+        running = jnp.dot(
+            causal.astype(jnp.float32),
+            log_decay,
+            precision=lax.Precision.HIGHEST,
+            preferred_element_type=jnp.float32,
+        )
+        running_rows = running.T
+        step_rows = step_size.T
+        affinity = jnp.where(causal, matmul(c_proj, b_proj, ((1,), (1,))), 0.0)
+        before = state[...]
+        before_high, before_low = split(before)
+        carried = matmul(c_proj, before_high) + matmul(c_proj, before_low)
+
+        left = lane < HEAD
+        for tile in range(SLOT // TILE):
+            span = slice(tile * TILE, (tile + 1) * TILE)
+            x = conved[:, span]
+            mixing, columns, steps = [], [], []
+            for half in range(2):
+                at = STATE + 2 * tile + half
+                column = jnp.broadcast_to(running[:, at : at + 1], (TILE, TILE))
+                decay = jnp.exp(jnp.minimum(column - running_rows[at : at + 1], 0.0))
+                mixing.append(decay * affinity * step_rows[at : at + 1])
+                columns.append(column)
+                steps.append(jnp.broadcast_to(step_size[:, at : at + 1], (TILE, TILE)))
+            weights, rest = split(jnp.concatenate(mixing, axis=1))
+            zero = jnp.zeros_like(x)
+            values = jnp.concatenate([jnp.where(left, x, zero), jnp.where(left, zero, x)], axis=0)
+            intra = matmul(weights, values) + matmul(rest, values)
+            run = jnp.where(left, columns[0], columns[1])
+            last = run[TILE - 1 :]
+            x32 = x.astype(jnp.float32)
+            result = intra + jnp.exp(run) * carried[:, span] + skip[:, span] * x32
+            z = gate[:, span]
+            gated = (result * (z * jax.nn.sigmoid(z))).astype(jnp.bfloat16)
+            width = min(out.shape[2] - tile * TILE, TILE)
+            for owner in range(TILE // own):
+                out[part * (TILE // own) + owner, :, tile * TILE : tile * TILE + width] = gated[
+                    owner * own : (owner + 1) * own, :width
+                ]
+            added = x32 * (jnp.exp(last - run) * jnp.where(left, steps[0], steps[1]))
+            added_high, added_low = split(added)
+            block = matmul(b_proj, added_high, ((0,), (0,))) + matmul(b_proj, added_low, ((0,), (0,)))
+            state[:, span] = jnp.exp(last) * before[:, span] + block
 
 
 def scan(tokens, weights, taps, conv_bias, head_rows, skip, own, width):
     positions, depth = tokens.shape
-    steps = positions // TILE
-    per_step = TILE // own
+    steps = positions // AHEAD
+    per_step = AHEAD // own
     whole = lambda array: pl.BlockSpec(array.shape, lambda i: (0,) * array.ndim)
     constants = (weights, taps, conv_bias, head_rows, skip)
     return pl.pallas_call(
         functools.partial(scan_kernel, own=own),
         grid=(steps + 1,),
-        in_specs=[pl.BlockSpec((TILE, depth), lambda i: (jnp.minimum(i, steps - 1), 0))]
+        in_specs=[pl.BlockSpec((AHEAD, depth), lambda i: (jnp.minimum(i, steps - 1), 0))]
         + [whole(array) for array in constants],
         out_specs=pl.BlockSpec((per_step, own, width), lambda i: (jnp.maximum(i - 1, 0), 0, 0)),
         out_shape=jax.ShapeDtypeStruct((positions // own, own, width), jnp.bfloat16),
         scratch_shapes=[
-            pltpu.VMEM((TILE, weights.shape[1]), jnp.bfloat16),
+            pltpu.VMEM((AHEAD, weights.shape[1]), jnp.bfloat16),
             pltpu.VMEM((TILE + 8, 2 * SLOT), jnp.float32),
             pltpu.VMEM((TILE, SLOT), jnp.float32),
         ],

time: 142 us -> 142 us (level)
  no operation moved by 1% of the time
where the time goes in v6:
time: 142 us; the launch traced here: 141 us
  waiting for transfers between devices  36 us (25%)
  Pallas kernels  30 us (21%)
  local copies, waits for them, and re-layouts  27.4 us (19%)
  other arithmetic  20.6 us (15%)
  between operations  14.3 us (10%)
  starting transfers between devices  12.9 us (9%)
    pallas_call x1, Pallas kernels, scan(): pl.pallas_call(functools.partial(scan_kernel, own=own), grid=(steps + 1,)...  27.3 us
    all_gather x1, waiting for transfers between devices, local(): gathered = lax.all_gather(own_rows, 'seq').reshape(owners * num_rows, depth)  16.8 us
    all_to_all x1, waiting for transfers between devices, local(): mine = lax.all_to_all(gated, 'seq', split_axis=0, concat_axis=0, tiled=True)  15.4 us
    ppermute x4, starting transfers between devices, around(): lax.ppermute(block, axis, [(i, (i + distance) % size) for i in range(size)])  7.5 us
    all_to_all x1, starting transfers between devices, local(): mine = lax.all_to_all(gated, 'seq', split_axis=0, concat_axis=0, tiled=True)  5.4 us
    unnamed x16, local copies, waits for them, and re-layouts  3.42 us
    another operation x2, other arithmetic, local(): jnp.stack([heads_of(dt_bias), heads_of(a_rate)])  3.23 us
    concatenate x1, other arithmetic, local(): jnp.concatenate([pad(both[:, :width], SLOT), pad(both[:, width:], SLOT),...  3.2 us
  transfers between devices with their start and end apart: 6, of which 3 were waited for; matrix products, arithmetic and copies ran while one was open for 33% of the time, Pallas kernels for 0%

profile of v6, /device:TPU:1, one launch (start us, length us, event | category | flops | bytes accessed | tf_op | source)
XLA Modules:
  0.0 141.2 jit_solution(12240293627405058672)
XLA Ops:
  8.7 1.2 copy.41
  10.6 2.0 %broadcast_in_dim.19 = bf16[3584,448]{1,0:T(8,128)(2,1)} broadcast(bf16[]{:T(256)} %constant.92.clone.1), dimensions={} | broadcast | bytes 3211266 | tf_op jit(solution)/shard_map/broadcast_in_dim | solution.py:186
  12.7 1.3 pad_maximum_fusion
  14.8 2.5 %collective-permute-start = (bf16[896,448]{0,1:T(8,128)(2,1)S(1)}, bf16[896,448]{0,1:T(8,128)(2,1)}, u32[]{:S(2)}, u32[]{:S(2)}) collective-permute-start(bf16[896,448]{0,1:T(8,128)(2,1)S(1)} %copy.44), channel_id=1, source_target_pairs={{0,32},{32,64},{64,96},{96,0},{1,33},{33,65},{65,97},{97,1},{2,34}... | collective-permute-start | bytes 2408456 | tf_op jit(solution)/shard_map/ppermute | solution.py:175
  17.3 2.2 %collective-permute-start.1 = (bf16[896,448]{0,1:T(8,128)(2,1)S(1)}, bf16[896,448]{0,1:T(8,128)(2,1)S(1)}, u32[]{:S(2)}, u32[]{:S(2)}) collective-permute-start(bf16[896,448]{0,1:T(8,128)(2,1)S(1)} %copy.44), channel_id=1, source_target_pairs={{0,96},{32,0},{64,32},{96,64},{1,97},{33,1},{65,33},{97,65},{2,98}... | collective-permute-start | bytes 2408456 | tf_op jit(solution)/shard_map/ppermute | solution.py:175
  28.3 1.3 constant_dynamic-slice_fusion.5
  30.4 1.4 maximum_select_fusion.3
  32.9 2.0 %constant_dynamic-slice_fusion.6 = (bf16[3584,64]{1,0:T(8,128)(2,1)S(1)}, bf16[3584,64]{1,0:T(8,128)(2,1)S(1)}) fusion(bf16[3584,256]{1,0:T(8,128)(2,1)} %param.15, s32[]{:T(128)S(6)} %select_n.152, s32[]{:T(128)S(6)} %select_n.151), kind=kLoop, calls=%fused_computation.39 | loop fusion | bytes 1835016 | tf_op jit(solution)/shard_map/dynamic_slice | solution.py:233
  35.5 1.9 %fusion.13 = (f32[1,4]{1,0:T(1,128)}, f32[1,4]{1,0:T(1,128)}) fusion(pred[]{:T(512)S(6)} %eq.19, f32[1]{0:T(128)} %slice.103, f32[3]{0:T(128)S(1)} %slice.102, f32[7]{0:T(128)S(1)} %dynamic_slice.45, f32[7]{0:T(128)S(1)} %dynamic_slice.46, f32[1]{0:T(128)} %slice.106, f32[3]{0:T(128)S(1)} %slice.105), kind=kLoop, calls=%fused_computation.53 | loop fusion | flops 16 | bytes 97 | tf_op jit(solution)/shard_map/stack | solution.py:258
  37.4 1.5 %fusion.9 = bf16[3584,128]{1,0:T(8,128)(2,1)} fusion(bf16[3584,4]{1,0:T(8,128)(2,1)S(1)} %copy.54, bf16[3584,64]{1,0:T(8,128)(2,1)S(1)} %get-tuple-element.5), kind=kLoop, calls=%fused_computation.15 | loop fusion | flops 3211264 | bytes 1404928 | tf_op jit(solution)/shard_map/concatenate | solution.py:245
  39.0 1.5 %copy.45 = bf16[896,448]{1,0:T(8,128)(2,1)S(1)} copy(bf16[896,448]{0,1:T(8,128)(2,1)} %collective-permute-done) | data formatting | bytes 1605632 | tf_op jit(solution)/shard_map/ppermute | solution.py:175
  42.1 2.7 %collective-permute-start.3 = (bf16[448,448]{1,0:T(8,128)(2,1)S(1)}, bf16[448,448]{1,0:T(8,128)(2,1)}, u32[]{:S(2)}, u32[]{:S(2)}) collective-permute-start(bf16[448,448]{1,0:T(8,128)(2,1)S(1)} %slice.118), channel_id=1, source_target_pairs={{0,96},{32,0},{64,32},{96,64},{1,97},{33,1},{65,33},{97,65},{2,98}... | collective-permute-start | bytes 1204232 | tf_op jit(solution)/shard_map/ppermute | solution.py:175
  44.8 1.3 select_maximum_fusion.2.head_rows
  47.5 1.3 select_maximum_fusion.taps
  50.8 3.1 %collective-permute-done.2 = bf16[448,448]{1,0:T(8,128)(2,1)} collective-permute-done((bf16[448,448]{1,0:T(8,128)(2,1)}, bf16[448,448]{1,0:T(8,128)(2,1)}, u32[]{:S(2)}, u32[]{:S(2)}) %collective-permute-start.2) | collective-permute-done | bytes 401440 | tf_op jit(solution)/shard_map/ppermute | solution.py:175
  53.9 2.2 %maximum_dynamic-update-slice_fusion = bf16[3584,448]{1,0:T(8,128)(2,1)} fusion(bf16[3584,448]{1,0:T(8,128)(2,1)} %constant_dynamic-update-slice_fusion, s32[]{:T(128)S(6)} %select_n.149, bf16[448,448]{1,0:T(8,128)(2,1)} %collective-permute-done.3, bf16[448,448]{1,0:T(8,128)(2,1)} %collective-permute-done.2), kind=kLoop, calls=%fused_computation.17 | loop fusion | flops 1605632 | bytes 1835012 | tf_op jit(solution)/shard_map/dynamic_update_slice | solution.py:188
  56.1 3.0 %slice.120 = bf16[3584,224]{1,0:T(8,128)(2,1)S(1)} slice(bf16[3584,448]{1,0:T(8,128)(2,1)} %maximum_dynamic-update-slice_fusion), slice={[0:3584], [224:448]} | slice | bytes 3211264 | tf_op jit(solution)/shard_map/slice | solution.py:243
  59.1 1.9 %slice_select_fusion = bf16[3584,256]{1,0:T(8,128)(2,1)S(1)} fusion(bf16[3584,448]{1,0:T(8,128)(2,1)} %maximum_dynamic-update-slice_fusion, pred[256]{0:T(512)(128)(4,1)S(1)} %copy-done.3), kind=kLoop, calls=%fused_computation.14 | loop fusion | flops 917504 | bytes 3670272 | tf_op jit(solution)/shard_map/jit(_pad)/pad | solution.py:223
  61.0 3.2 %fusion.5.weights = bf16[3584,768]{1,0:T(8,128)(2,1)} fusion(bf16[3584,64]{1,0:T(8,128)(2,1)S(1)} %get-tuple-element.6, bf16[3584,224]{1,0:T(8,128)(2,1)S(1)} %slice.120, bf16[3584,128]{1,0:T(8,128)(2,1)S(1)} %copy-done.1, bf16[3584,256]{1,0:T(8,128)(2,1)S(1)} %slice_select_fusion), kind=kLoop, calls=%fused_computation.9 | loop fusion | flops 44040192 | bytes 10321920 | tf_op jit(solution)/shard_map/concatenate | solution.py:240
  64.2 16.8 %all-gather.2.cloned.1.call-done = bf16[32,64,3584]{2,1,0:T(8,128)(2,1)} async-done(((bf16[1,64,3584]{2,1,0:T(8,128)(2,1)}), bf16[32,64,3584]{2,1,0:T(8,128)(2,1)}) %all-gather.2.cloned.1.call-update) | async-done | bytes 14680080 | tf_op jit(solution)/shard_map/all_gather | solution.py:217
  81.0 27.3 %mixer_scan.1 = bf16[32,64,224]{2,1,0:T(8,128)(2,1)} custom-call(bf16[2048,3584]{1,0:T(8,128)(2,1)} %bitcast.16, bf16[3584,768]{1,0:T(8,128)(2,1)} %fusion.5.weights, f32[4,512]{1,0:T(4,128)} %select_maximum_fusion.taps, f32[1,512]{1,0:T(1,128)} %fusion.12.conv_bias, f32[2,128]{1,0:T(2,128)} %select_maximum_fusion.2.head_rows, ...), custom_call_target="tpu_custom_call" | custom-call | tf_op jit(solution)/shard_map/mixer_scan/pallas_call | solution.py:118
  108.3 5.4 %all-to-all-start = ((bf16[32,64,224]{2,1,0:T(8,128)(2,1)}), bf16[32,64,224]{2,1,0:T(8,128)(2,1)S(1)}, u32[]{:S(2)}, u32[]{:S(2)}) async-start(bf16[32,64,224]{2,1,0:T(8,128)(2,1)} %mixer_scan.1), calls=%async_computation | async-start | bytes 2097152 | tf_op jit(solution)/shard_map/all_to_all | solution.py:267
  115.2 15.4 %all-to-all-done.gated = bf16[32,64,224]{2,1,0:T(8,128)(2,1)S(1)} async-done(((bf16[32,64,224]{2,1,0:T(8,128)(2,1)}), bf16[32,64,224]{2,1,0:T(8,128)(2,1)S(1)}, u32[]{:S(2)}, u32[]{:S(2)}) %all-to-all-start) | async-done | bytes 917536 | tf_op jit(solution)/shard_map/all_to_all | solution.py:267
  131.6 2.8 %gated_norm.1 = bf16[64,7168]{1,0:T(8,128)(2,1)} custom-call(s32[1]{0:T(128)S(6)} %sub.17.limit, bf16[32,64,224]{2,1,0:T(8,128)(2,1)} %copy-done, f32[32,224]{1,0:T(8,128)} %maximum_select_fusion.2.gain), custom_call_target="tpu_custom_call" | custom-call | tf_op jit(solution)/shard_map/gated_norm/pallas_call | solution.py:160
  (61 shorter events, 21.6 us)
Async XLA Ops:
  6.5 74.5 %all-gather.2.cloned.1.call-start = ((), (), s32[]{:S(2)}) async-start(), calls=%async_computation.1 | async-start | bytes 15138816 | tf_op jit(solution)/shard_map/all_gather | solution.py:217
  10.6 8.9 %copy-start.4 = (f32[112]{0:T(128)S(1)}, f32[112]{0:T(128)}, u32[]{:S(2)}) copy-start(f32[112]{0:T(128)} %param.17) | copy-start | bytes 1348
  10.6 9.7 %copy-start.5 = (f32[112]{0:T(128)S(1)}, f32[112]{0:T(128)}, u32[]{:S(2)}) copy-start(f32[112]{0:T(128)} %param.18) | copy-start | bytes 1348
  10.6 10.4 %copy-start.6 = (f32[112]{0:T(128)S(1)}, f32[112]{0:T(128)}, u32[]{:S(2)}) copy-start(f32[112]{0:T(128)} %param.21) | copy-start | bytes 1348
  14.8 24.2 %collective-permute-start = (bf16[896,448]{0,1:T(8,128)(2,1)S(1)}, bf16[896,448]{0,1:T(8,128)(2,1)}, u32[]{:S(2)}, u32[]{:S(2)}) collective-permute-start(bf16[896,448]{0,1:T(8,128)(2,1)S(1)} %copy.44), channel_id=1, source_target_pairs={{0,32},{32,64},{64,96},{96,0},{1,33},{33,65},{65,97},{97,1},{2,34}... | collective-permute-start | bytes 2408456 | tf_op jit(solution)/shard_map/ppermute | solution.py:175
  17.3 24.0 %collective-permute-start.1 = (bf16[896,448]{0,1:T(8,128)(2,1)S(1)}, bf16[896,448]{0,1:T(8,128)(2,1)S(1)}, u32[]{:S(2)}, u32[]{:S(2)}) collective-permute-start(bf16[896,448]{0,1:T(8,128)(2,1)S(1)} %copy.44), channel_id=1, source_target_pairs={{0,96},{32,0},{64,32},{96,64},{1,97},{33,1},{65,33},{97,65},{2,98}... | collective-permute-start | bytes 2408456 | tf_op jit(solution)/shard_map/ppermute | solution.py:175
  41.3 12.6 %collective-permute-start.2 = (bf16[448,448]{1,0:T(8,128)(2,1)}, bf16[448,448]{1,0:T(8,128)(2,1)}, u32[]{:S(2)}, u32[]{:S(2)}) collective-permute-start(bf16[448,448]{1,0:T(8,128)(2,1)} %slice.117), channel_id=1, source_target_pairs={{0,32},{32,64},{64,96},{96,0},{1,33},{33,65},{65,97},{97,1},{2,34}... | collective-permute-start | bytes 1204232 | tf_op jit(solution)/shard_map/ppermute | solution.py:175
  42.1 11.8 %collective-permute-start.3 = (bf16[448,448]{1,0:T(8,128)(2,1)S(1)}, bf16[448,448]{1,0:T(8,128)(2,1)}, u32[]{:S(2)}, u32[]{:S(2)}) collective-permute-start(bf16[448,448]{1,0:T(8,128)(2,1)S(1)} %slice.118), channel_id=1, source_target_pairs={{0,96},{32,0},{64,32},{96,64},{1,97},{33,1},{65,33},{97,65},{2,98}... | collective-permute-start | bytes 1204232 | tf_op jit(solution)/shard_map/ppermute | solution.py:175
  49.8 9.3 %copy-start.3 = (pred[256]{0:T(512)(128)(4,1)S(1)}, pred[256]{0:T(512)(128)(4,1)}, u32[]{:S(2)}) copy-start(pred[256]{0:T(512)(128)(4,1)} %constant.91.clone.1) | copy-start | bytes 772
  56.1 4.9 %copy-start.1 = (bf16[3584,128]{1,0:T(8,128)(2,1)S(1)}, bf16[3584,128]{1,0:T(8,128)(2,1)}, u32[]{:S(2)}) copy-start(bf16[3584,128]{1,0:T(8,128)(2,1)} %fusion.9) | copy-start | bytes 2752516
  81.0 32.7 %copy-start.2 = (f32[7168]{0:T(1024)S(1)}, f32[7168]{0:T(1024)}, u32[]{:S(2)}) copy-start(f32[7168]{0:T(1024)} %param.22) | copy-start | bytes 86020
  108.3 22.3 %all-to-all-start = ((bf16[32,64,224]{2,1,0:T(8,128)(2,1)}), bf16[32,64,224]{2,1,0:T(8,128)(2,1)S(1)}, u32[]{:S(2)}, u32[]{:S(2)}) async-start(bf16[32,64,224]{2,1,0:T(8,128)(2,1)} %mixer_scan.1), calls=%async_computation | async-start | bytes 2097152 | tf_op jit(solution)/shard_map/all_to_all | solution.py:267
  130.6 1.0 copy-start
Sparse Core Ops, SparseCore 0:
  9.6 71.3 all-gather.1
